TPU v7x, 256 devices: a whole 4x4x8 slice. The times are simulated.
256 devices in a mesh: region: 8 (over x, core), sub: 32 (over z, y).
Axes of the slice: x: 4, y: 4, z: 8, core: 2. Of those that a mesh axis runs over, the one named last changes fastest.
Arguments:
- observations: bfloat16 [262144, 256], P(('region', 'sub')), may hold values from -6 to 6
- basis_root: bfloat16 [262144, 512], P(('region', 'sub')), may hold values from -0.25 to 0.25
- basis_region: bfloat16 [262144, 512], P(('region', 'sub')), may hold values from -0.25 to 0.25
- noise_weights: float32 [262144], P(('region', 'sub')), may hold values from 0.3 to 4
- leaf_rows: int32 [256], P(('region', 'sub')), may hold values from 256 to 1024
- root_prior: float32 [512, 512], replicated, as said below
- region_prior: float32 [8, 512, 512], P('region'), as said below
Outputs:
- fitted: float32 [262144, 256], P(('region', 'sub'))
- root_mean: float32 [512, 256], replicated
Inputs may be any that keep to these rules, and one draw needn't show every extreme that they name: `root_prior`: symmetric positive definite. `region_prior`: each symmetric positive definite.
All inputs are finite; a program needn't handle non-finite values.
Results may differ from a plain program's by a relative error of at most 0.0041.
Values sent between devices are 32-bit elements; how exact they have to be, the bound alone decides.
A program may use at most 64 MiB of HBM per device.

v0:
```python
import jax
import jax.numpy as jnp
from jax import lax
from jax.sharding import PartitionSpec as P


def gram(left, right):
    return lax.dot_general(
        left, right, (((0,), (0,)), ((), ())), preferred_element_type=jnp.float32
    )


def hdot(a, b):
    return jnp.dot(a, b, precision=lax.Precision.HIGHEST)


def body(
    observations, basis_root, basis_region, noise_weights, leaf_rows, root_prior, region_prior
):
    slots = observations.shape[0]
    knots = basis_root.shape[1]
    live = jnp.arange(slots, dtype=jnp.int32) < leaf_rows[0]
    weight = jnp.where(live, noise_weights, jnp.zeros_like(noise_weights))
    weighted_root = (basis_root * weight[:, None]).astype(jnp.bfloat16)
    weighted_region = (basis_region * weight[:, None]).astype(jnp.bfloat16)
    g00 = gram(weighted_root, basis_root)
    g01 = gram(weighted_root, basis_region)
    g11 = gram(weighted_region, basis_region)
    o0 = gram(weighted_root, observations)
    o1 = gram(weighted_region, observations)
    prior = region_prior[0]
    a00, a01, a11, w0, w1 = lax.psum((g00, g01, g11, o0, o1), "sub")
    factor = jnp.linalg.cholesky(prior + a11)
    solved = jax.scipy.linalg.cho_solve((factor, True), jnp.concatenate([a01.T, w1], axis=1))
    schur = a00 - hdot(a01, solved[:, :knots])
    tail = w0 - hdot(a01, solved[:, knots:])
    schur_total, tail_total = lax.psum((schur, tail), "region")
    root_factor = jnp.linalg.cholesky(root_prior + schur_total)
    root_mean = jax.scipy.linalg.cho_solve((root_factor, True), tail_total)
    region_mean = solved[:, knots:] - hdot(solved[:, :knots], root_mean)
    fitted = jnp.dot(basis_root, root_mean.astype(jnp.bfloat16), preferred_element_type=jnp.float32)
    fitted = fitted + jnp.dot(
        basis_region, region_mean.astype(jnp.bfloat16), preferred_element_type=jnp.float32
    )
    return (fitted, root_mean)


def solution(mesh):
    placed = (
        P(("region", "sub"), None),
        P(("region", "sub"), None),
        P(("region", "sub"), None),
        P(("region", "sub")),
        P(("region", "sub")),
        P(),
        P("region", None, None),
    )
    return jax.shard_map(
        body,
        mesh=mesh,
        in_specs=placed,
        out_specs=(P(("region", "sub"), None), P()),
        check_vma=False,
    )
```

profile of v0, /device:TPU:1, one launch (start us, length us, event | category | flops | bytes accessed | tf_op | source)
XLA Modules:
  0.0 585.1 jit_solution(2302580666098274337)
XLA Ops:
  8.6 3.5 fusion.1
  20.4 164.0 %all-reduce.6.cloned.1.call-done = (f32[512,256]{1,0:T(8,128)}, f32[512,512]{1,0:T(8,128)}, f32[512,256]{0,1:T(8,128)}, f32[512,512]{0,1:T(8,128)}, f32[512,512]{0,1:T(8,128)}) async-done(((f32[512,256]{1,0:T(8,128)}, f32[512,512]{1,0:T(8,128)}, f32[512,256]{0,1:T(8,128)}, f32[512,512]{0,1:T(8,128)}, f32[512,512]{0,1:T(8,128)}), (f32[512,256]{1,0:T(8,128)}, f32[512,512]{1,0:T(8,128)}, f32[512,256]{0,1:T(8,128)}, ...) | async-done | bytes 4194320 | tf_op jit(solution)/shard_map/psum | solution.py:32
  187.4 11.7 %cholesky.286 = f32[128,128]{1,0:T(8,128)S(1)} custom-call(f32[128,128]{1,0:T(8,128)S(1)} %cholesky.426), custom_call_target="Cholesky" | custom-call | tf_op jit(solution)/shard_map/jit(cholesky)/cholesky | solution.py:33
  199.1 9.8 %custom-call.39 = f32[1,128,128]{1,2,0:T(8,128)S(1)} custom-call(f32[1,128,128]{2,1,0:T(8,128)S(1)} %get-tuple-element.67), custom_call_target="InvertDiagBlocksLowerTriangular" | custom-call | tf_op jit(solution)/shard_map/jit(cholesky)/cholesky | solution.py:33
  211.6 11.7 %cholesky.305 = f32[128,128]{1,0:T(8,128)S(1)} custom-call(f32[128,128]{1,0:T(8,128)S(1)} %cholesky.430), custom_call_target="Cholesky" | custom-call | tf_op jit(solution)/shard_map/jit(cholesky)/cholesky | solution.py:33
  223.3 10.2 %custom-call.40 = f32[1,128,128]{1,2,0:T(8,128)S(1)} custom-call(f32[1,128,128]{2,1,0:T(8,128)S(1)} %get-tuple-element.64), custom_call_target="InvertDiagBlocksLowerTriangular" | custom-call | tf_op jit(solution)/shard_map/jit(cholesky)/cholesky | solution.py:33
  235.1 11.7 %cholesky.326 = f32[128,128]{1,0:T(8,128)S(1)} custom-call(f32[128,128]{1,0:T(8,128)S(1)} %cholesky.435), custom_call_target="Cholesky" | custom-call | tf_op jit(solution)/shard_map/jit(cholesky)/cholesky | solution.py:33
  247.5 9.8 %custom-call.41 = f32[1,128,128]{1,2,0:T(8,128)S(1)} custom-call(f32[1,128,128]{2,1,0:T(8,128)S(1)} %get-tuple-element.61), custom_call_target="InvertDiagBlocksLowerTriangular" | custom-call | tf_op jit(solution)/shard_map/jit(cholesky)/cholesky | solution.py:33
  258.7 11.9 %cholesky.343 = f32[128,128]{1,0:T(8,128)S(1)} custom-call(f32[128,128]{1,0:T(8,128)S(1)} %convolution_subtract_fusion.20), custom_call_target="Cholesky" | custom-call | tf_op jit(solution)/shard_map/jit(cholesky)/cholesky | solution.py:33
  275.6 11.3 %while.2 = (s32[]{:T(128)}, f32[512,512]{1,0:T(8,128)}, s32[4,2]{0,1:T(2,128)S(1)}, f32[4,128,128]{2,1,0:T(8,128)S(1)}, s32[]{:T(128)}) while((s32[]{:T(128)}, f32[512,512]{1,0:T(8,128)}, s32[4,2]{0,1:T(2,128)S(1)}, f32[4,128,128]{2,1,0:T(8,128)S(1)}, s32[]{:T(128)}) %tuple.54), condition=%wide.while_cond, body=%wide.while_body.sunk | while | flops 2 | bytes 131181 | solution.py:34
  286.9 39.3 %custom-call.34 = f32[4,128,128]{1,2,0:T(8,128)S(1)} custom-call(f32[4,128,128]{2,1,0:T(8,128)S(1)} %get-tuple-element.10), custom_call_target="InvertDiagBlocksLowerTriangular" | custom-call | tf_op jit(solution)/shard_map/jit(_cho_solve)/triangular_solve | solution.py:34
  331.8 3.0 convolution_subtract_fusion.5
  344.8 3.3 convolution_subtract_fusion
  350.6 65.3 %all-reduce.8.cloned.1.call-done = (f32[512,256]{1,0:T(8,128)}, f32[512,512]{0,1:T(8,128)}) async-done(((f32[512,256]{1,0:T(8,128)}, f32[512,512]{0,1:T(8,128)}), (f32[512,256]{1,0:T(8,128)}, f32[512,512]{0,1:T(8,128)})) %all-reduce.8.cloned.1.call-update) | async-done | bytes 1572880 | tf_op jit(solution)/shard_map/psum | solution.py:37
  421.5 11.7 %cholesky.358 = f32[128,128]{1,0:T(8,128)S(1)} custom-call(f32[128,128]{1,0:T(8,128)S(1)} %cholesky.439), custom_call_target="Cholesky" | custom-call | tf_op jit(solution)/shard_map/jit(cholesky)/cholesky | solution.py:38
  433.4 9.8 %custom-call.42 = f32[1,128,128]{1,2,0:T(8,128)S(1)} custom-call(f32[1,128,128]{2,1,0:T(8,128)S(1)} %get-tuple-element.57), custom_call_target="InvertDiagBlocksLowerTriangular" | custom-call | tf_op jit(solution)/shard_map/jit(cholesky)/cholesky | solution.py:38
  445.7 11.9 %cholesky.377 = f32[128,128]{1,0:T(8,128)S(1)} custom-call(f32[128,128]{1,0:T(8,128)S(1)} %cholesky.443), custom_call_target="Cholesky" | custom-call | tf_op jit(solution)/shard_map/jit(cholesky)/cholesky | solution.py:38
  458.9 9.8 %custom-call.43 = f32[1,128,128]{1,2,0:T(8,128)S(1)} custom-call(f32[1,128,128]{2,1,0:T(8,128)S(1)} %get-tuple-element.54), custom_call_target="InvertDiagBlocksLowerTriangular" | custom-call | tf_op jit(solution)/shard_map/jit(cholesky)/cholesky | solution.py:38
  470.3 11.7 %cholesky.398 = f32[128,128]{1,0:T(8,128)S(1)} custom-call(f32[128,128]{1,0:T(8,128)S(1)} %cholesky.448), custom_call_target="Cholesky" | custom-call | tf_op jit(solution)/shard_map/jit(cholesky)/cholesky | solution.py:38
  482.8 9.8 %custom-call.44 = f32[1,128,128]{1,2,0:T(8,128)S(1)} custom-call(f32[1,128,128]{2,1,0:T(8,128)S(1)} %get-tuple-element.51), custom_call_target="InvertDiagBlocksLowerTriangular" | custom-call | tf_op jit(solution)/shard_map/jit(cholesky)/cholesky | solution.py:38
  494.0 11.9 %cholesky.415 = f32[128,128]{1,0:T(8,128)S(1)} custom-call(f32[128,128]{1,0:T(8,128)S(1)} %convolution_subtract_fusion.19), custom_call_target="Cholesky" | custom-call | tf_op jit(solution)/shard_map/jit(cholesky)/cholesky | solution.py:38
  511.0 14.1 %while.3 = (s32[]{:T(128)}, f32[512,512]{1,0:T(8,128)}, s32[4,2]{0,1:T(2,128)S(1)}, f32[4,128,128]{2,1,0:T(8,128)}, s32[]{:T(128)}) while((s32[]{:T(128)}, f32[512,512]{1,0:T(8,128)}, s32[4,2]{0,1:T(2,128)S(1)}, f32[4,128,128]{2,1,0:T(8,128)}, s32[]{:T(128)}) %tuple.66), condition=%wide.while_cond.1, body=%wide.while_body.1.sunk | while | flops 2 | bytes 132705 | solution.py:39
  511.6 2.9 bitcast_dynamic-update-slice_fusion.5
  525.0 40.2 %custom-call.35 = f32[4,128,128]{1,2,0:T(8,128)S(1)} custom-call(f32[4,128,128]{2,1,0:T(8,128)} %get-tuple-element.18), custom_call_target="InvertDiagBlocksLowerTriangular" | custom-call | tf_op jit(solution)/shard_map/jit(_cho_solve)/triangular_solve | solution.py:39
  (149 shorter events, 89.3 us)
Async XLA Ops:
  7.2 8.7 %copy-start = (bf16[1024,256]{1,0:T(8,128)(2,1)S(1)}, bf16[1024,256]{1,0:T(8,128)(2,1)}, u32[]{:S(2)}) copy-start(bf16[1024,256]{1,0:T(8,128)(2,1)} %param.8) | copy-start | bytes 1572868
  7.2 177.2 %all-reduce.6.cloned.1.call-start = ((), (), s32[]{:S(2)}) async-start(), calls=%async_computation | async-start | bytes 8388608 | tf_op jit(solution)/shard_map/psum | solution.py:32
  8.6 3.5 copy-start.11
  8.6 3.5 copy-start.13
  18.8 1.2 copy-start.9
  18.8 397.2 %all-reduce.8.cloned.1.call-start = ((), (), s32[]{:S(2)}) async-start(), calls=%async_computation.1 | async-start | bytes 3145728 | tf_op jit(solution)/shard_map/psum | solution.py:37
  186.4 1.0 copy-start.8
  274.5 51.8 %copy-start.1 = (f32[512,512]{1,0:T(8,128)S(1)}, f32[512,512]{1,0:T(8,128)}, u32[]{:S(2)}) copy-start(f32[512,512]{1,0:T(8,128)} %get-tuple-element.38) | copy-start | bytes 3145732
  274.5 51.8 %copy-start.4 = (f32[512,256]{0,1:T(8,128)S(1)}, f32[512,256]{0,1:T(8,128)}, u32[]{:S(2)}) copy-start(f32[512,256]{0,1:T(8,128)} %get-tuple-element.39) | copy-start | bytes 1572868
  341.9 1.1 copy-start.16
  342.0 2.8 copy-start.2
  343.0 1.8 copy-start.15
  348.1 1.2 copy-start.10
  420.5 1.0 copy-start.7
  525.0 44.5 %copy-start.6 = (f32[512,512]{1,0:T(8,128)S(1)}, f32[512,512]{1,0:T(8,128)}, u32[]{:S(2)}) copy-start(f32[512,512]{1,0:T(8,128)} %get-tuple-element.180) | copy-start | bytes 3145732
  572.0 1.5 copy-start.3
  573.5 1.0 copy-start.5
  573.6 1.4 copy-start.12
  575.0 1.2 copy-start.14
Sparse Core Ops, SparseCore 0:
  18.9 165.4 all-reduce.5
  348.2 67.7 all-reduce.7
where the time goes:
time: 591 us; the launch traced here: 585 us
  other arithmetic  246 us (42%)
  waiting for transfers between devices  229 us (39%)
  matrix products  51.8 us (9%)
  local copies, waits for them, and re-layouts  37.1 us (6%)
  between operations  20.7 us (4%)
    psum x1, waiting for transfers between devices, body(): a00, a01, a11, w0, w1 = lax.psum((g00, g01, g11, o0, o1), 'sub')  164 us
    another operation x15, other arithmetic, body(): root_factor = jnp.linalg.cholesky(root_prior + schur_total)  79.4 us
    another operation x14, other arithmetic, body(): factor = jnp.linalg.cholesky(prior + a11)  78.9 us
    psum x1, waiting for transfers between devices, body(): schur_total, tail_total = lax.psum((schur, tail), 'region')  65.3 us
    another operation x3, other arithmetic, body(): root_mean = jax.scipy.linalg.cho_solve((root_factor, True), tail_total)  41.3 us
    another operation x4, other arithmetic, body(): jax.scipy.linalg.cho_solve((factor, True), jnp.concatenate([a01.T, w1], a...  40.5 us
    another operation x24, local copies, waits for them, and re-layouts  25.3 us
    another operation x14, matrix products, body(): jax.scipy.linalg.cho_solve((factor, True), jnp.concatenate([a01.T, w1], a...  15.5 us
  transfers between devices with their start and end apart: 2, of which 2 were waited for; matrix products, arithmetic and copies ran while one was open for 0% of the time, Pallas kernels for 0%

commit v1 on v0

--- a/solution.py
+++ b/solution.py
@@ -1,7 +1,113 @@
 import jax
 import jax.numpy as jnp
 from jax import lax
+from jax.experimental import pallas as pl
+from jax.experimental.pallas import tpu as pltpu
 from jax.sharding import PartitionSpec as P
+
+F32 = jnp.float32
+BF16 = jnp.bfloat16
+HI = lax.Precision.HIGHEST
+
+def split(x):
+    hi = x.astype(BF16)
+    return hi, (x - hi.astype(F32)).astype(BF16)
+
+def dot3(a, b, dims):
+    ah, al = a
+    bh, bl = b
+    d = lambda u, v: lax.dot_general(u, v, (dims, ((), ())), preferred_element_type=F32)
+    return d(ah, bh) + (d(ah, bl) + d(al, bh))
+
+MM = ((1,), (0,))
+
+def inv_small(s):
+    s = dict(s)
+    g = lambda i, j: s[(i, j)] if i >= j else s[(j, i)]
+    for k in range(0, 8, 2):
+        a, b, c = g(k, k), g(k + 1, k), g(k + 1, k + 1)
+        r = 1.0 / (a * c - b * b)
+        d00, d01, d11 = c * r, -b * r, a * r
+        others = [i for i in range(8) if i not in (k, k + 1)]
+        t = {}
+        for i in others:
+            u, v = g(i, k), g(i, k + 1)
+            t[i] = (u * d00 + v * d01, u * d01 + v * d11)
+        new = {}
+        for i in others:
+            for j in others:
+                if i >= j:
+                    new[(i, j)] = g(i, j) - (t[i][0] * g(j, k) + t[i][1] * g(j, k + 1))
+        for i in others:
+            for q in (0, 1):
+                key = (max(i, k + q), min(i, k + q))
+                new[key] = t[i][q]
+        new[(k, k)], new[(k + 1, k)], new[(k + 1, k + 1)] = -d00, -d01, -d11
+        s = new
+    return {key: -v for key, v in s.items()}
+
+def inv128(rows):
+    lane = lax.broadcasted_iota(jnp.int32, (8, 128), 1)
+    sub = lax.broadcasted_iota(jnp.int32, (8, 128), 0)
+    a = list(rows)
+    for p in range(16):
+        R = a[p]
+        k0 = 8 * p
+        inK = (lane >= k0) & (lane < k0 + 8)
+        cols = [jnp.broadcast_to(R[:, k0 + j:k0 + j + 1], (8, 128)) for j in range(8)]
+        s = {(i, j): jnp.broadcast_to(cols[j][i:i + 1, :], (8, 128)) for i in range(8) for j in range(i + 1)}
+        Rm = jnp.where(inK, jnp.where(lane - k0 == sub, -1.0, 0.0), R)
+        Rb = [jnp.broadcast_to(Rm[q:q + 1, :], (8, 128)) for q in range(8)]
+        D = inv_small(s)
+        g = lambda i, j: D[(i, j)] if i >= j else D[(j, i)]
+        G = []
+        for i in range(8):
+            t = [g(i, q) * Rb[q] for q in range(8)]
+            while len(t) > 1:
+                t = [t[m] + t[m + 1] for m in range(0, len(t), 2)]
+            G.append(t[0])
+        order = [i % 16 for i in range(p + 1, p + 16)]
+        for i in order:
+            c = [jnp.broadcast_to(a[i][:, k0 + j:k0 + j + 1], (8, 128)) * G[j] for j in range(8)]
+            while len(c) > 1:
+                c = [c[m] + c[m + 1] for m in range(0, len(c), 2)]
+            a[i] = jnp.where(inK, 0.0, a[i]) - c[0]
+        new = G[7]
+        for q in range(7):
+            new = jnp.where(sub == q, G[q], new)
+        a[p] = new
+    return a
+
+def spd_inverse(A, Dbuf, n=512):
+    nb = n // 128
+    def step(k, carry):
+        o = pl.multiple_of(k * 128, 128)
+        rows = [A[pl.ds(pl.multiple_of(o + 8 * i, 8), 8), pl.ds(o, 128)] for i in range(16)]
+        out = inv128(rows)
+        for i in range(16):
+            Dbuf[8 * i:8 * i + 8, :] = -out[i]
+        D = split(Dbuf[...])
+        Rk = split(A[pl.ds(o, 128), :])
+        Ck = split(A[:, pl.ds(o, 128)])
+        G = dot3(D, Rk, MM)
+        T = dot3(Ck, D, MM)
+        U = dot3(Ck, split(G), MM)
+        A[...] = A[...] - U
+        A[pl.ds(o, 128), :] = G
+        A[:, pl.ds(o, 128)] = T
+        A[pl.ds(o, 128), pl.ds(o, 128)] = -Dbuf[...]
+        return carry
+    lax.fori_loop(0, nb, step, 0)
+
+def inverse_kernel(x_ref, o_ref, A, D):
+    A[...] = x_ref[...]
+    spd_inverse(A, D)
+    o_ref[...] = -A[...]
+
+def inverse(x):
+    return pl.pallas_call(inverse_kernel, out_shape=jax.ShapeDtypeStruct(x.shape, F32),
+        in_specs=[pl.BlockSpec(memory_space=pltpu.VMEM)], out_specs=pl.BlockSpec(memory_space=pltpu.VMEM),
+        scratch_shapes=[pltpu.VMEM((512, 512), F32), pltpu.VMEM((128, 128), F32)])(x)
 
 
 def gram(left, right):
@@ -28,15 +134,15 @@
     g11 = gram(weighted_region, basis_region)
     o0 = gram(weighted_root, observations)
     o1 = gram(weighted_region, observations)
-    prior = region_prior[0]
     a00, a01, a11, w0, w1 = lax.psum((g00, g01, g11, o0, o1), "sub")
-    factor = jnp.linalg.cholesky(prior + a11)
-    solved = jax.scipy.linalg.cho_solve((factor, True), jnp.concatenate([a01.T, w1], axis=1))
+    system = region_prior[0] + a11
+    region_inverse = inverse((system + system.T) * 0.5)
+    solved = hdot(region_inverse, jnp.concatenate([a01.T, w1], axis=1))
     schur = a00 - hdot(a01, solved[:, :knots])
     tail = w0 - hdot(a01, solved[:, knots:])
     schur_total, tail_total = lax.psum((schur, tail), "region")
-    root_factor = jnp.linalg.cholesky(root_prior + schur_total)
-    root_mean = jax.scipy.linalg.cho_solve((root_factor, True), tail_total)
+    root = root_prior + schur_total
+    root_mean = hdot(inverse((root + root.T) * 0.5), tail_total)
     region_mean = solved[:, knots:] - hdot(solved[:, :knots], root_mean)
     fitted = jnp.dot(basis_root, root_mean.astype(jnp.bfloat16), preferred_element_type=jnp.float32)
     fitted = fitted + jnp.dot(

time: 591 us -> 336 us (0.57)
  other arithmetic: 246 us -> 7.48 us
  Pallas kernels: 0 us -> 52 us
  local copies, waits for them, and re-layouts: 37.1 us -> 7.7 us
  matrix products: 51.8 us -> 23.2 us
    another operation x36 -> x0, other arithmetic: 240 us -> none  [the longest x15 79.4 us: body(): root_factor = jnp.linalg.cholesky(root_prior + schur_total)]
    pallas_call x0 -> x2, Pallas kernels: none -> 52 us  [inverse(): pl.pallas_call(inverse_kernel, out_shape=jax.ShapeDtypeStruct(x.shape, F3...]
    another operation x40 -> x0, matrix products: 34.6 us -> none  [the longest x14 15.5 us: body(): jax.scipy.linalg.cho_solve((factor, True), jnp.concatenate([a01.T, w1], a...]
    another operation x33 -> x0, local copies, waits for them, and re-layouts: 25.5 us -> none
    dot_general x3 -> x5, matrix products: 6.11 us -> 12.1 us  [hdot(): return jnp.dot(a, b, precision=lax.Precision.HIGHEST)]
where the time goes in v1:
time: 336 us; the launch traced here: 335 us
  waiting for transfers between devices  229 us (68%)
  Pallas kernels  52 us (15%)
  matrix products  23.2 us (7%)
  between operations  14.9 us (4%)
  local copies, waits for them, and re-layouts  7.7 us (2%)
  other arithmetic  7.48 us (2%)
    psum x1, waiting for transfers between devices, body(): a00, a01, a11, w0, w1 = lax.psum((g00, g01, g11, o0, o1), 'sub')  164 us
    psum x1, waiting for transfers between devices, body(): schur_total, tail_total = lax.psum((schur, tail), 'region')  65.5 us
    pallas_call x2, Pallas kernels, inverse(): pl.pallas_call(inverse_kernel, out_shape=jax.ShapeDtypeStruct(x.shape, F3...  52 us
    dot_general x5, matrix products, hdot(): return jnp.dot(a, b, precision=lax.Precision.HIGHEST)  12.1 us
    dot_general x5, matrix products, gram(): lax.dot_general(left, right, (((0,), (0,)), ((), ())), preferred_element_...  10.2 us
  transfers between devices with their start and end apart: 2, of which 2 were waited for; matrix products, arithmetic and copies ran while one was open for 0% of the time, Pallas kernels for 0%

profile of v1, /device:TPU:1, one launch (start us, length us, event | category | flops | bytes accessed | tf_op | source)
XLA Modules:
  0.0 334.7 jit_solution(493369174998326346)
XLA Ops:
  8.6 3.6 %fusion.5 = f32[512,512]{0,1:T(8,128)} fusion(bf16[1024,512]{1,0:T(8,128)(2,1)} %param.9, f32[1024]{0:T(1024)S(1)} %fusion.23), kind=kOutput, calls=%fused_computation.7 | convolution fusion | flops 538443776 | bytes 2101248 | tf_op jit(solution)/shard_map/dot_general | solution.py:114
  12.2 1.4 fusion.4
  13.7 1.5 fusion.7
  15.2 1.8 fusion.8
  17.0 1.8 fusion.9
  18.9 1.1 copy-done.3
  20.4 163.8 %all-reduce.5.cloned.1.call-done = (f32[512,512]{0,1:T(8,128)}, f32[512,512]{1,0:T(8,128)}, f32[512,512]{0,1:T(8,128)}, f32[512,256]{0,1:T(8,128)}, f32[512,256]{1,0:T(8,128)}) async-done(((f32[512,512]{0,1:T(8,128)}, f32[512,512]{1,0:T(8,128)}, f32[512,512]{0,1:T(8,128)}, f32[512,256]{0,1:T(8,128)}, f32[512,256]{1,0:T(8,128)}), (f32[512,512]{0,1:T(8,128)}, f32[512,512]{1,0:T(8,128)}, f32[512,512]{0,1:T(8,128)}, ...) | async-done | bytes 4194320 | tf_op jit(solution)/shard_map/psum | solution.py:137
  184.2 1.4 bitcast_add_fusion.2
  185.9 1.2 fusion.12.x_ref
  187.1 26.0 %shard_map.86 = f32[512,512]{1,0:T(8,128)} custom-call(f32[512,512]{1,0:T(8,128)} %fusion.12.x_ref), custom_call_target="tpu_custom_call" | custom-call | tf_op jit(solution)/shard_map/pallas_call | solution.py:108
  213.1 4.1 %fusion = f32[512,768]{1,0:T(8,128)S(1)} fusion(f32[512,512]{1,0:T(8,128)} %shard_map.86, f32[512,256]{0,1:T(8,128)} %get-tuple-element.7, f32[512,512]{0,1:T(8,128)S(1)} %bitcast.29), kind=kOutput, calls=%fused_computation.2 | convolution fusion | flops 2416312320 | bytes 4194304 | tf_op jit(solution)/shard_map/dot_general | solution.py:120
  217.3 1.8 convolution_subtract_fusion.2
  219.1 2.9 convolution_subtract_fusion
  222.0 1.2 copy-done.4
  223.2 1.3 copy.14
  224.5 65.5 %all-reduce.7.cloned.1.call-done = (f32[512,512]{0,1:T(8,128)}, f32[512,256]{1,0:T(8,128)}) async-done(((f32[512,512]{0,1:T(8,128)}, f32[512,256]{1,0:T(8,128)}), (f32[512,512]{0,1:T(8,128)}, f32[512,256]{1,0:T(8,128)})) %all-reduce.7.cloned.1.call-update) | async-done | bytes 1572880 | tf_op jit(solution)/shard_map/psum | solution.py:143
  290.0 1.7 add.34
  291.7 1.3 copy.15
  293.0 2.4 fusion.11.x_ref
  295.5 26.0 %shard_map.87 = f32[512,512]{1,0:T(8,128)} custom-call(f32[512,512]{1,0:T(8,128)} %fusion.11.x_ref), custom_call_target="tpu_custom_call" | custom-call | tf_op jit(solution)/shard_map/pallas_call | solution.py:108
  321.5 2.3 fusion.25
  323.8 1.0 fusion.10
  325.3 0.7 copy-done.8
  326.5 1.3 copy.16
  (30 shorter events, 2.5 us)
Async XLA Ops:
  7.2 5.1 %copy-start = (bf16[1024,256]{1,0:T(8,128)(2,1)S(1)}, bf16[1024,256]{1,0:T(8,128)(2,1)}, u32[]{:S(2)}) copy-start(bf16[1024,256]{1,0:T(8,128)(2,1)} %param.7) | copy-start | bytes 1572868
  7.2 177.0 %all-reduce.5.cloned.1.call-start = ((), (), s32[]{:S(2)}) async-start(), calls=%async_computation | async-start | bytes 8388608 | tf_op jit(solution)/shard_map/psum | solution.py:137
  8.6 3.6 %copy-start.7 = (bf16[1024,512]{1,0:T(8,128)(2,1)S(1)}, bf16[1024,512]{1,0:T(8,128)(2,1)}, u32[]{:S(2)}) copy-start(bf16[1024,512]{1,0:T(8,128)(2,1)} %param.9) | copy-start | bytes 3145732
  12.2 1.4 copy-start.5
  18.9 1.2 copy-start.3
  18.9 271.1 %all-reduce.7.cloned.1.call-start = ((), (), s32[]{:S(2)}) async-start(), calls=%async_computation.1 | async-start | bytes 3145728 | tf_op jit(solution)/shard_map/psum | solution.py:143
  187.1 26.0 %copy-start.1 = (f32[512,512]{1,0:T(8,128)S(1)}, f32[512,512]{1,0:T(8,128)}, u32[]{:S(2)}) copy-start(f32[512,512]{1,0:T(8,128)} %get-tuple-element.5) | copy-start | bytes 3145732
  213.1 4.2 %copy-start.10 = (f32[512,256]{1,0:T(8,128)S(1)}, f32[512,256]{1,0:T(8,128)}, u32[]{:S(2)}) copy-start(f32[512,256]{1,0:T(8,128)} %get-tuple-element.8) | copy-start | bytes 1572868
  217.3 1.8 copy-start.9
  221.9 1.2 copy-start.4
  295.5 26.0 %copy-start.11 = (f32[512,256]{1,0:T(8,128)S(1)}, f32[512,256]{1,0:T(8,128)}, u32[]{:S(2)}) copy-start(f32[512,256]{1,0:T(8,128)} %get-tuple-element.10) | copy-start | bytes 1572868
  321.5 3.3 copy-start.6
  323.8 1.5 copy-start.2
  324.8 1.2 copy-start.8
Sparse Core Ops, SparseCore 0:
  19.0 165.1 all-reduce.4
  222.1 67.8 all-reduce.6

commit v2 on v1

--- a/solution.py
+++ b/solution.py
@@ -1,3 +1,5 @@
+import functools
+
 import jax
 import jax.numpy as jnp
 from jax import lax
@@ -5,6 +7,7 @@
 from jax.experimental.pallas import tpu as pltpu
 from jax.sharding import PartitionSpec as P
 
+MESH = pl.DeviceIdType.MESH
 F32 = jnp.float32
 BF16 = jnp.bfloat16
 HI = lax.Precision.HIGHEST
@@ -78,11 +81,11 @@
         a[p] = new
     return a
 
-def spd_inverse(A, Dbuf, n=512):
+def spd_inverse(A, Dbuf, n=512, serve=None):
     nb = n // 128
     def step(k, carry):
-        o = pl.multiple_of(k * 128, 128)
-        rows = [A[pl.ds(pl.multiple_of(o + 8 * i, 8), 8), pl.ds(o, 128)] for i in range(16)]
+        o = k * 128 if serve is not None else pl.multiple_of(k * 128, 128)
+        rows = [A[pl.ds(o + 8 * i if serve is not None else pl.multiple_of(o + 8 * i, 8), 8), pl.ds(o, 128)] for i in range(16)]
         out = inv128(rows)
         for i in range(16):
             Dbuf[8 * i:8 * i + 8, :] = -out[i]
@@ -97,57 +100,332 @@
         A[:, pl.ds(o, 128)] = T
         A[pl.ds(o, 128), pl.ds(o, 128)] = -Dbuf[...]
         return carry
-    lax.fori_loop(0, nb, step, 0)
-
-def inverse_kernel(x_ref, o_ref, A, D):
-    A[...] = x_ref[...]
-    spd_inverse(A, D)
-    o_ref[...] = -A[...]
-
-def inverse(x):
-    return pl.pallas_call(inverse_kernel, out_shape=jax.ShapeDtypeStruct(x.shape, F32),
-        in_specs=[pl.BlockSpec(memory_space=pltpu.VMEM)], out_specs=pl.BlockSpec(memory_space=pltpu.VMEM),
-        scratch_shapes=[pltpu.VMEM((512, 512), F32), pltpu.VMEM((128, 128), F32)])(x)
-
-
-def gram(left, right):
-    return lax.dot_general(
-        left, right, (((0,), (0,)), ((), ())), preferred_element_type=jnp.float32
-    )
-
-
-def hdot(a, b):
-    return jnp.dot(a, b, precision=lax.Precision.HIGHEST)
+    if serve is None:
+        lax.fori_loop(0, nb, step, 0)
+    else:
+        for k in range(nb):
+            step(k, 0)
+            serve(k)
+
+
+NT = ((1,), (1,))
+TN = ((0,), (0,))
+
+
+class Copies:
+    def __init__(self, send_sems, recv_sems):
+        self.send_sems, self.recv_sems, self.used, self.sent = send_sems, recv_sems, 0, []
+
+    def slots(self, count):
+        first = self.used
+        self.used += count
+        return first
+
+    def start(self, source, target, slot, peer):
+        copy = pltpu.make_async_remote_copy(
+            src_ref=source, dst_ref=target, send_sem=self.send_sems.at[slot], recv_sem=self.recv_sems.at[slot],
+            device_id=peer, device_id_type=MESH,
+        )
+        copy.start()
+        self.sent.append(copy)
+        return copy
+
+    def finish(self):
+        for copy in self.sent:
+            copy.wait_send()
+        self.sent = []
+
+
+class Place:
+    def __init__(self):
+        self.r = lax.axis_index("region")
+        s = lax.axis_index("sub")
+        self.y, self.z = lax.rem(s, 4), s // 4
+        self.core = lax.rem(self.r, 2)
+        self.y1 = self.y + 1 - 2 * lax.rem(self.y, 2)
+        self.y3 = 3 - self.y
+        self.y2 = lax.rem(self.y + 2, 4)
+
+    def at_y(self, y):
+        return {"region": self.r, "sub": self.z * 4 + y}
+
+    def at_z(self, d):
+        return {"region": self.r, "sub": lax.rem(self.z + d, 8) * 4 + self.y}
+
+    def at_r(self, r):
+        return {"region": r, "sub": self.z * 4 + self.y}
+
+
+class Reduce:
+    def __init__(self, me, copies, x, r1, r2, zbuf, out):
+        self.me, self.copies, self.x, self.r1, self.r2, self.zbuf, self.out = me, copies, x, r1, r2, zbuf, out
+        self.first = [me.y1, me.y3]
+        self.second = [me.y3, me.y1]
+
+    def block(self, ref, h, b):
+        return ref.at[h, pl.ds(pl.multiple_of(b * 64, 64), 64), :]
+
+    def start(self):
+        me, c = self.me, self.copies
+        self.c1 = {}
+        for slot in (1, 0):
+            for h in (0, 1):
+                b = self.first[h] if slot == 0 else me.y2
+                self.c1[h, slot] = c.start(self.block(self.x, h, b), self.r1.at[h, slot], c.slots(1), me.at_y(self.first[h]))
+
+    def middle(self):
+        me, c = self.me, self.copies
+        self.c2 = {}
+        for h in (0, 1):
+            self.c1[h, 1].wait_recv()
+            self.r1[h, 1] = self.r1[h, 1] + self.block(self.x, h, self.second[h])[...]
+            self.c2[h] = c.start(self.r1.at[h, 1], self.r2.at[h], c.slots(1), me.at_y(self.second[h]))
+
+    def across(self):
+        me, c = self.me, self.copies
+        for h in (0, 1):
+            self.c1[h, 0].wait_recv()
+            self.c2[h].wait_recv()
+            self.r1[h, 0] = self.r1[h, 0] + self.block(self.x, h, me.y)[...] + self.r2[h]
+        self.cz = []
+        for d in (4, 3, 5, 2, 6, 1, 7):
+            row = pl.multiple_of(lax.rem(me.z + d, 8) * 8, 8)
+            self.cz.append(c.start(self.r1.at[:, 0, pl.ds(row, 8), :], self.zbuf.at[d - 1], c.slots(1), me.at_z(d)))
+
+    def end(self):
+        row = pl.multiple_of(self.me.z * 8, 8)
+        for copy in self.cz:
+            copy.wait_recv()
+        for h in (0, 1):
+            total = self.r1[h, 0, pl.ds(row, 8), :]
+            for d in range(7):
+                total = total + self.zbuf[d, h]
+            self.out[h] = total
+
+
+class Gather:
+    def __init__(self, me, copies, slab, full):
+        self.me, self.copies, self.slab, self.full = me, copies, slab, full
+
+    def block(self, h, b):
+        return self.full.at[h, pl.ds(pl.multiple_of(b * 64, 64), 64), :]
+
+    def start(self):
+        me, c = self.me, self.copies
+        row = pl.multiple_of(me.y * 64 + me.z * 8, 8)
+        self.full[:, pl.ds(row, 8), :] = self.slab[...]
+        piece = self.full.at[:, pl.ds(row, 8), :]
+        self.cz = [c.start(self.slab, piece, c.slots(1), me.at_z(d)) for d in (4, 3, 5, 2, 6, 1, 7)]
+
+    def middle(self):
+        me, c = self.me, self.copies
+        for copy in self.cz:
+            copy.wait_recv()
+        self.c1, self.c2 = [], []
+        for h, near, far in ((0, me.y3, me.y1), (1, me.y1, me.y3)):
+            own = self.block(h, me.y)
+            self.c1.append(c.start(own, own, c.slots(1), me.at_y(near)))
+            self.c2.append(c.start(own, own, c.slots(1), me.at_y(far)))
+
+    def last(self):
+        me, c = self.me, self.copies
+        for h, near, far in ((0, me.y3, me.y1), (1, me.y1, me.y3)):
+            self.c1[h].wait_recv()
+            passed = self.block(h, near)
+            self.c2.append(c.start(passed, passed, c.slots(1), me.at_y(far)))
+
+    def end(self):
+        for copy in self.c2:
+            copy.wait_recv()
+
+
+class RootSum:
+    def __init__(self, me, copies, slab, rx, own, full):
+        self.me, self.copies, self.slab, self.rx, self.own, self.full = me, copies, slab, rx, own, full
+
+    def run(self):
+        me, c = self.me, self.copies
+        slot = c.slots(8)
+        for d in range(1, 8):
+            peer = lax.rem(me.r + d, 8)
+            copy = pltpu.make_async_remote_copy(
+                src_ref=self.slab.at[lax.rem(peer, 2)], dst_ref=self.rx.at[me.r],
+                send_sem=c.send_sems.at[slot + d - 1], recv_sem=c.recv_sems.at[slot + me.r],
+                device_id=me.at_r(peer), device_id_type=MESH,
+            )
+            copy.start()
+            c.sent.append(copy)
+        self.rx[me.r] = self.slab[me.core]
+        for d in range(1, 8):
+            peer = lax.rem(me.r + d, 8)
+            pltpu.make_async_remote_copy(
+                src_ref=self.slab.at[0], dst_ref=self.rx.at[peer],
+                send_sem=c.send_sems.at[slot + d - 1], recv_sem=c.recv_sems.at[slot + peer],
+                device_id=me.at_r(peer), device_id_type=MESH,
+            ).wait_recv()
+        total = self.rx[0]
+        for i in range(1, 8):
+            total = total + self.rx[i]
+        self.own[...] = total
+        row = pl.multiple_of(me.y * 64 + me.z * 8, 8)
+        self.full[me.core, pl.ds(row, 8), :] = total
+        piece = self.full.at[me.core, pl.ds(row, 8), :]
+        cz = [c.start(self.own, piece, c.slots(1), me.at_z(d)) for d in (4, 3, 5, 2, 6, 1, 7)]
+        for copy in cz:
+            copy.wait_recv()
+        near = me.y3 + me.core * (me.y1 - me.y3)
+        far = me.y1 + me.core * (me.y3 - me.y1)
+        sibling = me.at_r(me.r + 1 - 2 * me.core)
+
+        def block(b):
+            return self.full.at[me.core, pl.ds(pl.multiple_of(b * 64, 64), 64), :]
+
+        own = block(me.y)
+        c1 = c.start(own, own, c.slots(1), me.at_y(near))
+        c2 = c.start(own, own, c.slots(1), me.at_y(far))
+        cs = [c.start(own, own, c.slots(1), sibling)]
+        c1.wait_recv()
+        passed = block(near)
+        c3 = c.start(passed, passed, c.slots(1), me.at_y(far))
+        cs.append(c.start(passed, passed, c.slots(1), sibling))
+        c2.wait_recv()
+        cs.append(c.start(block(far), block(far), c.slots(1), sibling))
+        c3.wait_recv()
+        cs.append(c.start(block(me.y2), block(me.y2), c.slots(1), sibling))
+        for copy in cs:
+            copy.wait_recv()
+
+
+def both(ref, cols):
+    return jnp.concatenate([ref[0, :, cols], ref[1, :, cols]], axis=0)
+
+
+def main_kernel(
+    rows_ref, obs, b0, b1, noise, root_prior, region_prior, root_out, region_low,
+    xa, xb, xc, w0, w1, r1a, r2a, za, sa, fa, r1b, r2b, zb, sb, fb, r1c, r2c, zc, sc, slab, rx, own, full,
+    inv_a, inv_d, x0, send_sems, recv_sems,
+):
+    me = Place()
+    copies = Copies(send_sems, recv_sems)
+    barrier = pltpu.get_barrier_semaphore()
+    for peer in [me.at_y(me.y1), me.at_y(me.y3)] + [me.at_z(d) for d in range(1, 8)] + [
+        me.at_r(lax.rem(me.r + d, 8)) for d in range(1, 8)
+    ]:
+        pl.semaphore_signal(barrier, inc=1, device_id=peer, device_id_type=MESH)
+
+    count = rows_ref[0]
+    lane = lax.broadcasted_iota(jnp.int32, (1, 128), 1)
+    for g in range(8):
+        wrow = jnp.where(lane + 128 * g < count, noise[g:g + 1, :], 0.0)
+        wt = jnp.broadcast_to(wrow, (128, 128)).T
+        for q in range(4):
+            rows, cols = slice(128 * g, 128 * g + 128), slice(128 * q, 128 * q + 128)
+            w1[rows, cols] = (b1[rows, cols].astype(F32) * wt).astype(BF16)
+            w0[rows, cols] = (b0[rows, cols].astype(F32) * wt).astype(BF16)
+
+    def dot(a, b):
+        return lax.dot_general(a, b, (TN, ((), ())), preferred_element_type=F32)
+
+    for h in (0, 1):
+        half = slice(256 * h, 256 * h + 256)
+        xa[h] = 0.5 * (dot(w1[:, half], b1[...]) + dot(b1[:, half], w1[...]))
+    pl.semaphore_wait(barrier, 16)
+    red_a = Reduce(me, copies, xa, r1a, r2a, za, sa)
+    red_a.start()
+    for h in (0, 1):
+        half = slice(256 * h, 256 * h + 256)
+        xb[h, :, :512] = dot(w0[:, half], b1[...])
+        xb[h, :, 512:] = dot(w1[:, half], obs[...])
+    red_a.middle()
+    red_b = Reduce(me, copies, xb, r1b, r2b, zb, sb)
+    red_b.start()
+    for h in (0, 1):
+        half = slice(256 * h, 256 * h + 256)
+        xc[h, :, :512] = 0.5 * (dot(w0[:, half], b0[...]) + dot(b0[:, half], w0[...]))
+        xc[h, :, 512:] = dot(w0[:, half], obs[...])
+    red_a.across()
+    red_c = Reduce(me, copies, xc, r1c, r2c, zc, sc)
+    red_c.start()
+    red_b.middle()
+    red_a.end()
+    gat_a = Gather(me, copies, sa, fa)
+    gat_a.start()
+    red_b.across()
+    red_c.middle()
+    gat_a.middle()
+    gat_a.last()
+    red_b.end()
+    gat_b = Gather(me, copies, sb, fb)
+    gat_b.start()
+    red_c.across()
+    gat_a.end()
+    for h in (0, 1):
+        half = slice(256 * h, 256 * h + 256)
+        inv_a[half, :] = region_prior[half, :] + fa[h]
+
+    def serve(k):
+        if k == 0:
+            gat_b.middle()
+        elif k == 1:
+            gat_b.last()
+        elif k == 2:
+            red_c.end()
+            gat_b.end()
+
+    spd_inverse(inv_a, inv_d, serve=serve)
+    P3 = split(-inv_a[...])
+    u = dot3(split(sb[...].reshape(16, 768)[:, :512]), P3, MM)
+    u3 = split(u)
+    a01 = split(both(fb, slice(0, 512)))
+    w13 = split(both(fb, slice(512, 768)))
+    s = sc[...].reshape(16, 768)[:, :512] - dot3(u3, a01, NT)
+    t = sc[...].reshape(16, 768)[:, 512:] - dot3(u3, w13, MM)
+    slab[:, :, :512] = s.reshape(2, 8, 512)
+    slab[:, :, 512:] = t.reshape(2, 8, 256)
+    root = RootSum(me, copies, slab, rx, own, full)
+    root.run()
+    x0[:, :512] = dot3(P3, a01, NT)
+    x0[:, 512:] = dot3(P3, w13, MM)
+    for h in (0, 1):
+        half = slice(256 * h, 256 * h + 256)
+        inv_a[half, :] = root_prior[half, :] + full[h, :, :512]
+    spd_inverse(inv_a, inv_d)
+    mean = dot3(split(-inv_a[...]), split(both(full, slice(512, 768))), MM)
+    root_out[...] = mean
+    region_low[...] = (x0[:, 512:] - dot3(split(x0[:, :512]), split(mean), MM)).astype(BF16)
+    copies.finish()
+
+
+def estimate(observations, basis_root, basis_region, noise_weights, leaf_rows, root_prior, region_prior):
+    vm = lambda *shape: pltpu.VMEM(shape, F32)
+
+    def reduce_set(w):
+        return [vm(2, 2, 64, w), vm(2, 64, w), vm(7, 2, 8, w), vm(2, 8, w)]
+
+    spec = pl.BlockSpec(memory_space=pltpu.VMEM)
+    return pl.pallas_call(
+        main_kernel,
+        out_shape=(jax.ShapeDtypeStruct((512, 256), F32), jax.ShapeDtypeStruct((512, 256), BF16)),
+        in_specs=[pl.BlockSpec(memory_space=pltpu.SMEM)] + [spec] * 6,
+        out_specs=(spec, spec),
+        scratch_shapes=[vm(2, 256, 512), vm(2, 256, 768), vm(2, 256, 768),
+                        pltpu.VMEM((1024, 512), BF16), pltpu.VMEM((1024, 512), BF16)]
+        + reduce_set(512) + [vm(2, 256, 512)] + reduce_set(768) + [vm(2, 256, 768)] + reduce_set(768)
+        + [vm(2, 8, 768), vm(8, 8, 768), vm(8, 768), vm(2, 256, 768)]
+        + [vm(512, 512), vm(128, 128), vm(512, 768)]
+        + [pltpu.SemaphoreType.DMA((100,)), pltpu.SemaphoreType.DMA((100,))],
+        compiler_params=pltpu.CompilerParams(collective_id=0, has_side_effects=True, vmem_limit_bytes=60 << 20),
+    )(leaf_rows, observations, basis_root, basis_region, noise_weights.reshape(8, 128), root_prior, region_prior[0])
 
 
 def body(
     observations, basis_root, basis_region, noise_weights, leaf_rows, root_prior, region_prior
 ):
-    slots = observations.shape[0]
-    knots = basis_root.shape[1]
-    live = jnp.arange(slots, dtype=jnp.int32) < leaf_rows[0]
-    weight = jnp.where(live, noise_weights, jnp.zeros_like(noise_weights))
-    weighted_root = (basis_root * weight[:, None]).astype(jnp.bfloat16)
-    weighted_region = (basis_region * weight[:, None]).astype(jnp.bfloat16)
-    g00 = gram(weighted_root, basis_root)
-    g01 = gram(weighted_root, basis_region)
-    g11 = gram(weighted_region, basis_region)
-    o0 = gram(weighted_root, observations)
-    o1 = gram(weighted_region, observations)
-    a00, a01, a11, w0, w1 = lax.psum((g00, g01, g11, o0, o1), "sub")
-    system = region_prior[0] + a11
-    region_inverse = inverse((system + system.T) * 0.5)
-    solved = hdot(region_inverse, jnp.concatenate([a01.T, w1], axis=1))
-    schur = a00 - hdot(a01, solved[:, :knots])
-    tail = w0 - hdot(a01, solved[:, knots:])
-    schur_total, tail_total = lax.psum((schur, tail), "region")
-    root = root_prior + schur_total
-    root_mean = hdot(inverse((root + root.T) * 0.5), tail_total)
-    region_mean = solved[:, knots:] - hdot(solved[:, :knots], root_mean)
+    root_mean, region_low = estimate(
+        observations, basis_root, basis_region, noise_weights, leaf_rows, root_prior, region_prior
+    )
     fitted = jnp.dot(basis_root, root_mean.astype(jnp.bfloat16), preferred_element_type=jnp.float32)
-    fitted = fitted + jnp.dot(
-        basis_region, region_mean.astype(jnp.bfloat16), preferred_element_type=jnp.float32
-    )
+    fitted = fitted + jnp.dot(basis_region, region_low, preferred_element_type=jnp.float32)
     return (fitted, root_mean)
 
 

time: 336 us -> 152 us (0.45)
  waiting for transfers between devices: 229 us -> 0 us
  Pallas kernels: 52 us -> 146 us
  matrix products: 23.2 us -> 2.11 us
  between operations: 14.9 us -> 1.36 us
  other arithmetic: 7.48 us -> 0 us
  local copies, waits for them, and re-layouts: 7.7 us -> 2.12 us
    psum x2 -> x0, waiting for transfers between devices: 229 us -> none  [the longest x1 164 us: body(): a00, a01, a11, w0, w1 = lax.psum((g00, g01, g11, o0, o1), 'sub')]
    pallas_call x2 -> x1, Pallas kernels: 52 us -> 146 us  [estimate(): pl.pallas_call(main_kernel, out_shape=(jax.ShapeDtypeStruct((512, 256), F...]
    dot_general x11 -> x1, matrix products: 22.8 us -> 0.49 us  [body(): jnp.dot(basis_region, region_low, preferred_element_type=jnp.float32)]
    unnamed x27 -> x10, local copies, waits for them, and re-layouts: 6.06 us -> 2.12 us
    mul x2 -> x0, other arithmetic: 3.61 us -> none  [the longest x1 2.41 us: body(): root_mean = hdot(inverse((root + root.T) * 0.5), tail_total)]
  transfers between devices with their start and end apart: 2 -> 0, of which waited for: 2 -> 0; matrix products, arithmetic and copies ran while one was open for 0% -> 0% of each run, Pallas kernels for 0% -> 0%
where the time goes in v2:
time: 152 us; the launch traced here: 151 us
  Pallas kernels  146 us (96%)
  local copies, waits for them, and re-layouts  2.12 us (1%)
  matrix products  2.11 us (1%)
    pallas_call x1, Pallas kernels, estimate(): pl.pallas_call(main_kernel, out_shape=(jax.ShapeDtypeStruct((512, 256), F...  146 us

profile of v2, /device:TPU:1, one launch (start us, length us, event | category | flops | bytes accessed | tf_op | source)
XLA Modules:
  0.0 151.2 jit_solution(15279193335242670829)
XLA Ops:
  1.3 0.0 copy-start
  1.3 145.6 %shard_map.86 = (f32[512,256]{1,0:T(8,128)}, bf16[512,256]{1,0:T(8,128)(2,1)}) custom-call(s32[1]{0:T(128)S(6)} %copy.11.rows_ref, bf16[1024,256]{1,0:T(8,128)(2,1)} %obs.1, bf16[1024,512]{1,0:T(8,128)(2,1)} %b0.1, bf16[1024,512]{1,0:T(8,128)(2,1)} %b1.1, f32[8,128]{1,0:T(8,128)} %bitcast.8, f32[512,512]{1,0:T(8,128)} %root_prior.1, f32[512,512]{1,0:T(8,128)} %bitcast.7), custom_call_target="tpu_custom_call" | custom-call | tf_op jit(solution)/shard_map/pallas_call | solution.py:406
  146.9 0.0 copy-done
  146.9 0.0 copy-start.1
  146.9 0.0 copy-start.3
  146.9 1.6 %fusion.1 = f32[256,1024]{1,0:T(8,128)S(1)} fusion(bf16[1024,512]{1,0:T(8,128)(2,1)S(1)} %copy-done, f32[512,256]{1,0:T(8,128)} %get-tuple-element.11), kind=kOutput, calls=%fused_computation.2 | convolution fusion | flops 268566528 | bytes 2621440 | tf_op jit(solution)/shard_map/dot_general | solution.py:427
  148.5 0.0 copy-done.1
  148.6 0.0 copy-done.3
  148.6 0.5 fusion
  149.1 0.0 copy-start.2
  149.1 1.3 copy.9
  150.4 0.0 copy-done.2
  150.4 0.8 copy.12
Async XLA Ops:
  1.3 145.6 %copy-start = (bf16[1024,512]{1,0:T(8,128)(2,1)S(1)}, bf16[1024,512]{1,0:T(8,128)(2,1)}, u32[]{:S(2)}) copy-start(bf16[1024,512]{1,0:T(8,128)(2,1)} %b0.1) | copy-start | bytes 3145732
  146.9 1.7 %copy-start.1 = (bf16[1024,512]{1,0:T(8,128)(2,1)S(1)}, bf16[1024,512]{1,0:T(8,128)(2,1)}, u32[]{:S(2)}) copy-start(bf16[1024,512]{1,0:T(8,128)(2,1)} %b1.1) | copy-start | bytes 3145732
  146.9 1.7 %copy-start.3 = (bf16[512,256]{1,0:T(8,128)(2,1)S(1)}, bf16[512,256]{1,0:T(8,128)(2,1)}, u32[]{:S(2)}) copy-start(bf16[512,256]{1,0:T(8,128)(2,1)} %get-tuple-element.5) | copy-start | bytes 786436
  149.1 1.3 copy-start.2

commit v3 on v2

--- a/solution.py
+++ b/solution.py
@@ -49,18 +49,23 @@
         s = new
     return {key: -v for key, v in s.items()}
 
-def inv128(rows):
+def inv128(rows, tmp, serve=None, base=0):
     lane = lax.broadcasted_iota(jnp.int32, (8, 128), 1)
     sub = lax.broadcasted_iota(jnp.int32, (8, 128), 0)
     a = list(rows)
     for p in range(16):
+        if serve is not None:
+            serve(base + p)
         R = a[p]
         k0 = 8 * p
         inK = (lane >= k0) & (lane < k0 + 8)
         cols = [jnp.broadcast_to(R[:, k0 + j:k0 + j + 1], (8, 128)) for j in range(8)]
-        s = {(i, j): jnp.broadcast_to(cols[j][i:i + 1, :], (8, 128)) for i in range(8) for j in range(i + 1)}
+        for j in range(8):
+            tmp[8 * j:8 * j + 8, :] = cols[j]
+        s = {(i, j): tmp[pl.ds(8 * j + i, 8, stride=0), :] for i in range(8) for j in range(i + 1)}
         Rm = jnp.where(inK, jnp.where(lane - k0 == sub, -1.0, 0.0), R)
-        Rb = [jnp.broadcast_to(Rm[q:q + 1, :], (8, 128)) for q in range(8)]
+        tmp[64:72, :] = Rm
+        Rb = [tmp[pl.ds(64 + q, 8, stride=0), :] for q in range(8)]
         D = inv_small(s)
         g = lambda i, j: D[(i, j)] if i >= j else D[(j, i)]
         G = []
@@ -69,15 +74,23 @@
             while len(t) > 1:
                 t = [t[m] + t[m + 1] for m in range(0, len(t), 2)]
             G.append(t[0])
-        order = [i % 16 for i in range(p + 1, p + 16)]
-        for i in order:
+        new = G[7]
+        for q in range(7):
+            new = jnp.where(sub == q, G[q], new)
+        Rh, Gh = R.astype(BF16).astype(F32), new.astype(BF16).astype(F32)
+        Rl, Gl = R - Rh, new - Gh
+        left = jnp.concatenate([Rh, Rh, Rl, Rl], axis=0).astype(BF16)
+        right = jnp.concatenate([Gh, Gl, Gh, Gl], axis=0).astype(BF16)
+        if p < 15:
+            i = p + 1
             c = [jnp.broadcast_to(a[i][:, k0 + j:k0 + j + 1], (8, 128)) * G[j] for j in range(8)]
             while len(c) > 1:
                 c = [c[m] + c[m + 1] for m in range(0, len(c), 2)]
             a[i] = jnp.where(inK, 0.0, a[i]) - c[0]
-        new = G[7]
-        for q in range(7):
-            new = jnp.where(sub == q, G[q], new)
+        U = lax.dot_general(left, right, (((0,), (0,)), ((), ())), preferred_element_type=F32)
+        for i in range(16):
+            if i != p and i != p + 1:
+                a[i] = jnp.where(inK, 0.0, a[i]) - U[8 * i:8 * i + 8, :]
         a[p] = new
     return a
 
@@ -86,7 +99,7 @@
     def step(k, carry):
         o = k * 128 if serve is not None else pl.multiple_of(k * 128, 128)
         rows = [A[pl.ds(o + 8 * i if serve is not None else pl.multiple_of(o + 8 * i, 8), 8), pl.ds(o, 128)] for i in range(16)]
-        out = inv128(rows)
+        out = inv128(rows, Dbuf, serve, 16 * k)
         for i in range(16):
             Dbuf[8 * i:8 * i + 8, :] = -out[i]
         D = split(Dbuf[...])
@@ -105,7 +118,6 @@
     else:
         for k in range(nb):
             step(k, 0)
-            serve(k)
 
 
 NT = ((1,), (1,))
@@ -187,20 +199,38 @@
             self.c1[h, 0].wait_recv()
             self.c2[h].wait_recv()
             self.r1[h, 0] = self.r1[h, 0] + self.block(self.x, h, me.y)[...] + self.r2[h]
-        self.cz = []
-        for d in (4, 3, 5, 2, 6, 1, 7):
-            row = pl.multiple_of(lax.rem(me.z + d, 8) * 8, 8)
-            self.cz.append(c.start(self.r1.at[:, 0, pl.ds(row, 8), :], self.zbuf.at[d - 1], c.slots(1), me.at_z(d)))
+        self.cz = [[], []]
+        self.c_step(0)
+
+    def chunk(self, d):
+        row = pl.multiple_of(lax.rem(self.me.z + d + 8, 8) * 8, 8)
+        return self.r1.at[:, 0, pl.ds(row, 8), :]
+
+    def c_step(self, step):
+        me, c = self.me, self.copies
+        for side, way in ((0, 1), (1, -1)):
+            part = self.chunk(way * (4 - step))
+            slot = 4 * side + step
+            if step == 0:
+                source, target = part.at[side], self.zbuf.at[slot, side]
+            else:
+                source, target = part, self.zbuf.at[slot]
+            self.cz[side].append(c.start(source, target, c.slots(1), me.at_z(1 if side == 0 else 7)))
+
+    def pass_on(self, step):
+        for side, way in ((0, 1), (1, -1)):
+            self.cz[side][step - 1].wait_recv()
+            part, slot = self.chunk(way * (4 - step)), 4 * side + step - 1
+            if step == 1:
+                part[side] = part[side] + self.zbuf[slot, side]
+            else:
+                part[...] = part[...] + self.zbuf[slot]
+        self.c_step(step)
 
     def end(self):
-        row = pl.multiple_of(self.me.z * 8, 8)
-        for copy in self.cz:
-            copy.wait_recv()
-        for h in (0, 1):
-            total = self.r1[h, 0, pl.ds(row, 8), :]
-            for d in range(7):
-                total = total + self.zbuf[d, h]
-            self.out[h] = total
+        for side in (0, 1):
+            self.cz[side][3].wait_recv()
+        self.out[...] = self.chunk(0)[...] + self.zbuf[3] + self.zbuf[7]
 
 
 class Gather:
@@ -214,13 +244,27 @@
         me, c = self.me, self.copies
         row = pl.multiple_of(me.y * 64 + me.z * 8, 8)
         self.full[:, pl.ds(row, 8), :] = self.slab[...]
-        piece = self.full.at[:, pl.ds(row, 8), :]
-        self.cz = [c.start(self.slab, piece, c.slots(1), me.at_z(d)) for d in (4, 3, 5, 2, 6, 1, 7)]
+        self.cz = [[], []]
+        self.send(0)
+
+    def send(self, step):
+        me, c = self.me, self.copies
+        for side, way in ((0, -1), (1, 1)):
+            row = pl.multiple_of(me.y * 64 + lax.rem(me.z + way * step + 8, 8) * 8, 8)
+            piece = self.full.at[:, pl.ds(row, 8), :]
+            if step == 3:
+                piece = piece.at[side]
+            self.cz[side].append(c.start(piece, piece, c.slots(1), me.at_z(1 if side == 0 else 7)))
+
+    def pass_on(self, step):
+        for side in (0, 1):
+            self.cz[side][step - 1].wait_recv()
+        self.send(step)
 
     def middle(self):
         me, c = self.me, self.copies
-        for copy in self.cz:
-            copy.wait_recv()
+        for side in (0, 1):
+            self.cz[side][3].wait_recv()
         self.c1, self.c2 = [], []
         for h, near, far in ((0, me.y3, me.y1), (1, me.y1, me.y3)):
             own = self.block(h, me.y)
@@ -243,7 +287,7 @@
     def __init__(self, me, copies, slab, rx, own, full):
         self.me, self.copies, self.slab, self.rx, self.own, self.full = me, copies, slab, rx, own, full
 
-    def run(self):
+    def run(self, fill):
         me, c = self.me, self.copies
         slot = c.slots(8)
         for d in range(1, 8):
@@ -271,6 +315,7 @@
         self.full[me.core, pl.ds(row, 8), :] = total
         piece = self.full.at[me.core, pl.ds(row, 8), :]
         cz = [c.start(self.own, piece, c.slots(1), me.at_z(d)) for d in (4, 3, 5, 2, 6, 1, 7)]
+        fill(0)
         for copy in cz:
             copy.wait_recv()
         near = me.y3 + me.core * (me.y1 - me.y3)
@@ -284,6 +329,7 @@
         c1 = c.start(own, own, c.slots(1), me.at_y(near))
         c2 = c.start(own, own, c.slots(1), me.at_y(far))
         cs = [c.start(own, own, c.slots(1), sibling)]
+        fill(1)
         c1.wait_recv()
         passed = block(near)
         c3 = c.start(passed, passed, c.slots(1), me.at_y(far))
@@ -343,39 +389,48 @@
         half = slice(256 * h, 256 * h + 256)
         xc[h, :, :512] = 0.5 * (dot(w0[:, half], b0[...]) + dot(b0[:, half], w0[...]))
         xc[h, :, 512:] = dot(w0[:, half], obs[...])
+    red_c = Reduce(me, copies, xc, r1c, r2c, zc, sc)
     red_a.across()
-    red_c = Reduce(me, copies, xc, r1c, r2c, zc, sc)
-    red_c.start()
-    red_b.middle()
+    for step in (1, 2, 3):
+        red_a.pass_on(step)
     red_a.end()
     gat_a = Gather(me, copies, sa, fa)
+    gat_b = Gather(me, copies, sb, fb)
     gat_a.start()
+    red_b.middle()
+    red_c.start()
+    for step in (1, 2, 3):
+        gat_a.pass_on(step)
+    gat_a.middle()
     red_b.across()
-    red_c.middle()
-    gat_a.middle()
+    red_b.pass_on(1)
     gat_a.last()
-    red_b.end()
-    gat_b = Gather(me, copies, sb, fb)
-    gat_b.start()
-    red_c.across()
+    red_b.pass_on(2)
     gat_a.end()
     for h in (0, 1):
         half = slice(256 * h, 256 * h + 256)
         inv_a[half, :] = region_prior[half, :] + fa[h]
-
-    def serve(k):
-        if k == 0:
-            gat_b.middle()
-        elif k == 1:
-            gat_b.last()
-        elif k == 2:
-            red_c.end()
-            gat_b.end()
+    tasks = {
+        2: [lambda: red_b.pass_on(3)],
+        6: [red_c.middle],
+        10: [red_b.end, gat_b.start],
+        18: [lambda: gat_b.pass_on(1)],
+        25: [red_c.across, lambda: gat_b.pass_on(2)],
+        33: [lambda: red_c.pass_on(1), lambda: gat_b.pass_on(3)],
+        41: [gat_b.middle, lambda: red_c.pass_on(2)],
+        50: [lambda: red_c.pass_on(3)],
+        58: [gat_b.last, red_c.end],
+    }
+
+    def serve(point):
+        for task in tasks.get(point, []):
+            task()
 
     spd_inverse(inv_a, inv_d, serve=serve)
     P3 = split(-inv_a[...])
     u = dot3(split(sb[...].reshape(16, 768)[:, :512]), P3, MM)
     u3 = split(u)
+    gat_b.end()
     a01 = split(both(fb, slice(0, 512)))
     w13 = split(both(fb, slice(512, 768)))
     s = sc[...].reshape(16, 768)[:, :512] - dot3(u3, a01, NT)
@@ -383,9 +438,14 @@
     slab[:, :, :512] = s.reshape(2, 8, 512)
     slab[:, :, 512:] = t.reshape(2, 8, 256)
     root = RootSum(me, copies, slab, rx, own, full)
-    root.run()
-    x0[:, :512] = dot3(P3, a01, NT)
-    x0[:, 512:] = dot3(P3, w13, MM)
+
+    def fill(part):
+        if part == 0:
+            x0[:, :512] = dot3(P3, a01, NT)
+        else:
+            x0[:, 512:] = dot3(P3, w13, MM)
+
+    root.run(fill)
     for h in (0, 1):
         half = slice(256 * h, 256 * h + 256)
         inv_a[half, :] = root_prior[half, :] + full[h, :, :512]
@@ -400,7 +460,7 @@
     vm = lambda *shape: pltpu.VMEM(shape, F32)
 
     def reduce_set(w):
-        return [vm(2, 2, 64, w), vm(2, 64, w), vm(7, 2, 8, w), vm(2, 8, w)]
+        return [vm(2, 2, 64, w), vm(2, 64, w), vm(8, 2, 8, w), vm(2, 8, w)]
 
     spec = pl.BlockSpec(memory_space=pltpu.VMEM)
     return pl.pallas_call(
@@ -413,7 +473,7 @@
         + reduce_set(512) + [vm(2, 256, 512)] + reduce_set(768) + [vm(2, 256, 768)] + reduce_set(768)
         + [vm(2, 8, 768), vm(8, 8, 768), vm(8, 768), vm(2, 256, 768)]
         + [vm(512, 512), vm(128, 128), vm(512, 768)]
-        + [pltpu.SemaphoreType.DMA((100,)), pltpu.SemaphoreType.DMA((100,))],
+        + [pltpu.SemaphoreType.DMA((112,)), pltpu.SemaphoreType.DMA((112,))],
         compiler_params=pltpu.CompilerParams(collective_id=0, has_side_effects=True, vmem_limit_bytes=60 << 20),
     )(leaf_rows, observations, basis_root, basis_region, noise_weights.reshape(8, 128), root_prior, region_prior[0])
 

time: 152 us -> 148 us (0.974)
  Pallas kernels: 146 us -> 142 us
    pallas_call x1, Pallas kernels: 146 us -> 142 us  [estimate(): pl.pallas_call(main_kernel, out_shape=(jax.ShapeDtypeStruct((512, 256), F...]
where the time goes in v3:
time: 148 us
  Pallas kernels  142 us (96%)
  local copies, waits for them, and re-layouts  2.12 us (1%)
  matrix products  2.11 us (1%)
    pallas_call x1, Pallas kernels, estimate(): pl.pallas_call(main_kernel, out_shape=(jax.ShapeDtypeStruct((512, 256), F...  142 us

profile of v3, /device:TPU:1, one launch (start us, length us, event | category | flops | bytes accessed | tf_op | source)
XLA Modules:
  0.0 147.7 jit_solution(11864961885924701071)
XLA Ops:
  1.3 0.0 copy-start
  1.3 142.2 %shard_map.86 = (f32[512,256]{1,0:T(8,128)}, bf16[512,256]{1,0:T(8,128)(2,1)}) custom-call(s32[1]{0:T(128)S(6)} %copy.11.rows_ref, bf16[1024,256]{1,0:T(8,128)(2,1)} %obs.1, bf16[1024,512]{1,0:T(8,128)(2,1)} %b0.1, bf16[1024,512]{1,0:T(8,128)(2,1)} %b1.1, f32[8,128]{1,0:T(8,128)} %bitcast.8, f32[512,512]{1,0:T(8,128)} %root_prior.1, f32[512,512]{1,0:T(8,128)} %bitcast.7), custom_call_target="tpu_custom_call" | custom-call | tf_op jit(solution)/shard_map/pallas_call | solution.py:466
  143.4 0.0 copy-done
  143.5 0.0 copy-start.1
  143.5 0.0 copy-start.3
  143.5 1.6 %fusion.1 = f32[256,1024]{1,0:T(8,128)S(1)} fusion(bf16[1024,512]{1,0:T(8,128)(2,1)S(1)} %copy-done, f32[512,256]{1,0:T(8,128)} %get-tuple-element.11), kind=kOutput, calls=%fused_computation.2 | convolution fusion | flops 268566528 | bytes 2621440 | tf_op jit(solution)/shard_map/dot_general | solution.py:487
  145.1 0.0 copy-done.1
  145.1 0.0 copy-done.3
  145.1 0.5 fusion
  145.6 0.0 copy-start.2
  145.6 1.3 copy.9
  146.9 0.0 copy-done.2
  146.9 0.8 copy.12
Async XLA Ops:
  1.3 142.2 %copy-start = (bf16[1024,512]{1,0:T(8,128)(2,1)S(1)}, bf16[1024,512]{1,0:T(8,128)(2,1)}, u32[]{:S(2)}) copy-start(bf16[1024,512]{1,0:T(8,128)(2,1)} %b0.1) | copy-start | bytes 3145732
  143.5 1.7 %copy-start.1 = (bf16[1024,512]{1,0:T(8,128)(2,1)S(1)}, bf16[1024,512]{1,0:T(8,128)(2,1)}, u32[]{:S(2)}) copy-start(bf16[1024,512]{1,0:T(8,128)(2,1)} %b1.1) | copy-start | bytes 3145732
  143.5 1.7 %copy-start.3 = (bf16[512,256]{1,0:T(8,128)(2,1)S(1)}, bf16[512,256]{1,0:T(8,128)(2,1)}, u32[]{:S(2)}) copy-start(bf16[512,256]{1,0:T(8,128)(2,1)} %get-tuple-element.5) | copy-start | bytes 786436
  145.6 1.3 copy-start.2

commit v4 on v3

--- a/solution.py
+++ b/solution.py
@@ -168,56 +168,68 @@
         return {"region": r, "sub": self.z * 4 + self.y}
 
 
-class Reduce:
-    def __init__(self, me, copies, x, r1, r2, zbuf, out):
-        self.me, self.copies, self.x, self.r1, self.r2, self.zbuf, self.out = me, copies, x, r1, r2, zbuf, out
-        self.first = [me.y1, me.y3]
-        self.second = [me.y3, me.y1]
-
-    def block(self, ref, h, b):
-        return ref.at[h, pl.ds(pl.multiple_of(b * 64, 64), 64), :]
-
-    def start(self):
+class Ring:
+    def rows(self, d):
+        return pl.ds(pl.multiple_of(lax.rem(self.me.z + d + 8, 8) * 8, 8), 8)
+
+    def up_or_down(self, side):
+        return self.me.at_z(1 if side == 0 else 7)
+
+
+class Reduce(Ring):
+    def __init__(self, me, copies, x, cols, y_first, r1, r2, zbuf, part, out):
+        self.me, self.copies, self.x, self.cols, self.y_first = me, copies, x, cols, y_first
+        self.r1, self.r2, self.zbuf, self.part, self.out = r1, r2, zbuf, part, out
+        self.first, self.second = [me.y1, me.y3], [me.y3, me.y1]
+        self.c1, self.c2, self.cz = {}, {}, [[], []]
+        ring = [self.z_start, lambda: self.z_pass(1), lambda: self.z_pass(2), lambda: self.z_pass(3)]
+        if y_first:
+            self.steps = [self.y_start, self.y_middle, lambda: (self.y_end(), ring[0]())] + ring[1:] + [self.z_end]
+        else:
+            self.steps = ring + [lambda: (self.z_end(), self.y_start()), self.y_middle, self.y_end]
+
+    def block(self, h, b):
+        return self.x.at[h, b, :, self.cols] if self.y_first else self.part.at[h, b]
+
+    def y_start(self):
         me, c = self.me, self.copies
-        self.c1 = {}
         for slot in (1, 0):
             for h in (0, 1):
                 b = self.first[h] if slot == 0 else me.y2
-                self.c1[h, slot] = c.start(self.block(self.x, h, b), self.r1.at[h, slot], c.slots(1), me.at_y(self.first[h]))
-
-    def middle(self):
+                self.c1[h, slot] = c.start(self.block(h, b), self.r1.at[h, slot], c.slots(1), me.at_y(self.first[h]))
+
+    def y_middle(self):
         me, c = self.me, self.copies
-        self.c2 = {}
         for h in (0, 1):
             self.c1[h, 1].wait_recv()
-            self.r1[h, 1] = self.r1[h, 1] + self.block(self.x, h, self.second[h])[...]
+            self.r1[h, 1] = self.r1[h, 1] + self.block(h, self.second[h])[...]
             self.c2[h] = c.start(self.r1.at[h, 1], self.r2.at[h], c.slots(1), me.at_y(self.second[h]))
 
-    def across(self):
-        me, c = self.me, self.copies
+    def y_end(self):
         for h in (0, 1):
             self.c1[h, 0].wait_recv()
             self.c2[h].wait_recv()
-            self.r1[h, 0] = self.r1[h, 0] + self.block(self.x, h, me.y)[...] + self.r2[h]
-        self.cz = [[], []]
-        self.c_step(0)
+            total = self.r1[h, 0] + self.block(h, self.me.y)[...] + self.r2[h]
+            if self.y_first:
+                self.r1[h, 0] = total
+            else:
+                self.out[h, :, self.cols] = total
 
     def chunk(self, d):
-        row = pl.multiple_of(lax.rem(self.me.z + d + 8, 8) * 8, 8)
-        return self.r1.at[:, 0, pl.ds(row, 8), :]
-
-    def c_step(self, step):
-        me, c = self.me, self.copies
+        return self.r1.at[:, 0, self.rows(d), :] if self.y_first else self.x.at[:, :, self.rows(d), self.cols]
+
+    def z_send(self, step):
+        c = self.copies
         for side, way in ((0, 1), (1, -1)):
-            part = self.chunk(way * (4 - step))
-            slot = 4 * side + step
+            source, target = self.chunk(way * (4 - step)), self.zbuf.at[4 * side + step]
             if step == 0:
-                source, target = part.at[side], self.zbuf.at[slot, side]
-            else:
-                source, target = part, self.zbuf.at[slot]
-            self.cz[side].append(c.start(source, target, c.slots(1), me.at_z(1 if side == 0 else 7)))
-
-    def pass_on(self, step):
+                source, target = source.at[side], target.at[side]
+            self.cz[side].append(c.start(source, target, c.slots(1), self.up_or_down(side)))
+
+    def z_start(self):
+        self.z_send(0)
+
+    def z_pass(self, step):
         for side, way in ((0, 1), (1, -1)):
             self.cz[side][step - 1].wait_recv()
             part, slot = self.chunk(way * (4 - step)), 4 * side + step - 1
@@ -225,62 +237,84 @@
                 part[side] = part[side] + self.zbuf[slot, side]
             else:
                 part[...] = part[...] + self.zbuf[slot]
-        self.c_step(step)
-
-    def end(self):
+        self.z_send(step)
+
+    def z_end(self):
         for side in (0, 1):
             self.cz[side][3].wait_recv()
-        self.out[...] = self.chunk(0)[...] + self.zbuf[3] + self.zbuf[7]
-
-
-class Gather:
-    def __init__(self, me, copies, slab, full):
-        self.me, self.copies, self.slab, self.full = me, copies, slab, full
+        total = self.chunk(0)[...] + self.zbuf[3] + self.zbuf[7]
+        if self.y_first:
+            self.out[:, :, self.cols] = total
+        else:
+            self.part[...] = total
+
+
+class Gather(Ring):
+    def __init__(self, me, copies, slab, full, cols, y_first):
+        self.me, self.copies, self.slab, self.full, self.cols, self.y_first = me, copies, slab, full, cols, y_first
+        self.c1, self.c2, self.cz = [], [], [[], []]
+        ring = [lambda: self.z_send(0), lambda: self.z_pass(1), lambda: self.z_pass(2), lambda: self.z_pass(3)]
+        if y_first:
+            self.steps = [lambda: (self.place(), self.y_start()), self.y_pass, lambda: (self.y_end(), ring[0]())]
+            self.steps += ring[1:] + [self.z_end]
+        else:
+            self.steps = [lambda: (self.place(), ring[0]())] + ring[1:]
+            self.steps += [lambda: (self.z_end(), self.y_start()), self.y_pass, self.y_end]
+
+    def place(self):
+        self.full[:, self.me.y, self.rows(0), self.cols] = self.slab[:, :, self.cols]
 
     def block(self, h, b):
-        return self.full.at[h, pl.ds(pl.multiple_of(b * 64, 64), 64), :]
-
-    def start(self):
+        return self.full.at[h, b, self.rows(0), self.cols] if self.y_first else self.full.at[h, b, :, self.cols]
+
+    def chunk(self, d):
+        if self.y_first:
+            return self.full.at[:, :, self.rows(d), self.cols]
+        return self.full.at[:, self.me.y, self.rows(d), self.cols]
+
+    def y_start(self):
         me, c = self.me, self.copies
-        row = pl.multiple_of(me.y * 64 + me.z * 8, 8)
-        self.full[:, pl.ds(row, 8), :] = self.slab[...]
-        self.cz = [[], []]
-        self.send(0)
-
-    def send(self, step):
-        me, c = self.me, self.copies
-        for side, way in ((0, -1), (1, 1)):
-            row = pl.multiple_of(me.y * 64 + lax.rem(me.z + way * step + 8, 8) * 8, 8)
-            piece = self.full.at[:, pl.ds(row, 8), :]
-            if step == 3:
-                piece = piece.at[side]
-            self.cz[side].append(c.start(piece, piece, c.slots(1), me.at_z(1 if side == 0 else 7)))
-
-    def pass_on(self, step):
-        for side in (0, 1):
-            self.cz[side][step - 1].wait_recv()
-        self.send(step)
-
-    def middle(self):
-        me, c = self.me, self.copies
-        for side in (0, 1):
-            self.cz[side][3].wait_recv()
-        self.c1, self.c2 = [], []
         for h, near, far in ((0, me.y3, me.y1), (1, me.y1, me.y3)):
             own = self.block(h, me.y)
             self.c1.append(c.start(own, own, c.slots(1), me.at_y(near)))
             self.c2.append(c.start(own, own, c.slots(1), me.at_y(far)))
 
-    def last(self):
+    def y_pass(self):
         me, c = self.me, self.copies
         for h, near, far in ((0, me.y3, me.y1), (1, me.y1, me.y3)):
             self.c1[h].wait_recv()
             passed = self.block(h, near)
             self.c2.append(c.start(passed, passed, c.slots(1), me.at_y(far)))
 
-    def end(self):
+    def y_end(self):
         for copy in self.c2:
             copy.wait_recv()
+
+    def z_send(self, step):
+        c = self.copies
+        for side, way in ((0, -1), (1, 1)):
+            piece = self.chunk(way * step)
+            if step == 3:
+                piece = piece.at[side]
+            self.cz[side].append(c.start(piece, piece, c.slots(1), self.up_or_down(side)))
+
+    def z_pass(self, step):
+        for side in (0, 1):
+            self.cz[side][step - 1].wait_recv()
+        self.z_send(step)
+
+    def z_end(self):
+        for side in (0, 1):
+            self.cz[side][3].wait_recv()
+
+
+class Both:
+    def __init__(self, *halves):
+        self.halves = halves
+
+    def __call__(self, step):
+        for half in self.halves:
+            half.steps[step]()
 
 
 class RootSum:
@@ -343,14 +377,16 @@
 
 
 def both(ref, cols):
-    return jnp.concatenate([ref[0, :, cols], ref[1, :, cols]], axis=0)
+    return jnp.concatenate([ref[h, ..., cols].reshape(256, -1) for h in (0, 1)], axis=0)
 
 
 def main_kernel(
     rows_ref, obs, b0, b1, noise, root_prior, region_prior, root_out, region_low,
-    xa, xb, xc, w0, w1, r1a, r2a, za, sa, fa, r1b, r2b, zb, sb, fb, r1c, r2c, zc, sc, slab, rx, own, full,
-    inv_a, inv_d, x0, send_sems, recv_sems,
+    xa, xb, xc, w0, w1, *rest,
 ):
+    sets, rest = [rest[9 * i:9 * i + 9] for i in range(3)], rest[27:]
+    fa, fb, slab, rx, own, full, inv_a, inv_d, x0, send_sems, recv_sems = rest
+    sa, sb, sc = [refs[8] for refs in sets]
     me = Place()
     copies = Copies(send_sems, recv_sems)
     barrier = pltpu.get_barrier_semaphore()
@@ -372,65 +408,59 @@
     def dot(a, b):
         return lax.dot_general(a, b, (TN, ((), ())), preferred_element_type=F32)
 
-    for h in (0, 1):
-        half = slice(256 * h, 256 * h + 256)
-        xa[h] = 0.5 * (dot(w1[:, half], b1[...]) + dot(b1[:, half], w1[...]))
+    def put(ref, h, cols, value):
+        ref[h, :, :, cols] = value.reshape(4, 64, value.shape[1])
+
+    def reduction(x, refs):
+        half = x.shape[3] // 2
+        y_side, z_side, out = refs[:4], refs[4:8], refs[8]
+        return Both(
+            Reduce(me, copies, x, slice(0, half), True, y_side[0], y_side[1], y_side[2], None, out),
+            Reduce(me, copies, x, slice(half, 2 * half), False, z_side[0], z_side[1], z_side[2], z_side[3], out),
+        )
+
+    def gathering(part, whole):
+        half = whole.shape[3] // 2
+        return Both(
+            Gather(me, copies, part, whole, slice(0, half), False),
+            Gather(me, copies, part, whole, slice(half, 2 * half), True),
+        )
+
+    halves = [(0, slice(0, 256)), (1, slice(256, 512))]
+    for h, half in halves:
+        put(xa, h, slice(0, 512), 0.5 * (dot(w1[:, half], b1[...]) + dot(b1[:, half], w1[...])))
     pl.semaphore_wait(barrier, 16)
-    red_a = Reduce(me, copies, xa, r1a, r2a, za, sa)
-    red_a.start()
-    for h in (0, 1):
-        half = slice(256 * h, 256 * h + 256)
-        xb[h, :, :512] = dot(w0[:, half], b1[...])
-        xb[h, :, 512:] = dot(w1[:, half], obs[...])
-    red_a.middle()
-    red_b = Reduce(me, copies, xb, r1b, r2b, zb, sb)
-    red_b.start()
-    for h in (0, 1):
-        half = slice(256 * h, 256 * h + 256)
-        xc[h, :, :512] = 0.5 * (dot(w0[:, half], b0[...]) + dot(b0[:, half], w0[...]))
-        xc[h, :, 512:] = dot(w0[:, half], obs[...])
-    red_c = Reduce(me, copies, xc, r1c, r2c, zc, sc)
-    red_a.across()
-    for step in (1, 2, 3):
-        red_a.pass_on(step)
-    red_a.end()
-    gat_a = Gather(me, copies, sa, fa)
-    gat_b = Gather(me, copies, sb, fb)
-    gat_a.start()
-    red_b.middle()
-    red_c.start()
-    for step in (1, 2, 3):
-        gat_a.pass_on(step)
-    gat_a.middle()
-    red_b.across()
-    red_b.pass_on(1)
-    gat_a.last()
-    red_b.pass_on(2)
-    gat_a.end()
-    for h in (0, 1):
-        half = slice(256 * h, 256 * h + 256)
-        inv_a[half, :] = region_prior[half, :] + fa[h]
+    red_a, red_b, red_c = [reduction(x, refs) for x, refs in zip((xa, xb, xc), sets)]
+    gat_a, gat_b = gathering(sa, fa), gathering(sb, fb)
+    red_a(0)
+    for h, half in halves:
+        put(xb, h, slice(0, 512), dot(w0[:, half], b1[...]))
+        put(xb, h, slice(512, 768), dot(w1[:, half], obs[...]))
+    red_a(1)
+    red_b(0)
+    for h, half in halves:
+        put(xc, h, slice(0, 512), 0.5 * (dot(w0[:, half], b0[...]) + dot(b0[:, half], w0[...])))
+        put(xc, h, slice(512, 768), dot(w0[:, half], obs[...]))
+    for step in (red_a, 2), (red_a, 3), (red_b, 1), (red_a, 4), (red_a, 5), (red_b, 2), (red_a, 6), (gat_a, 0), \
+            (red_b, 3), (gat_a, 1), (gat_a, 2), (red_b, 4), (gat_a, 3), (red_c, 0), (gat_a, 4), (red_b, 5), \
+            (gat_a, 5), (red_b, 6), (gat_b, 0), (gat_a, 6):
+        step[0](step[1])
+    for h, half in halves:
+        inv_a[half, :] = region_prior[half, :] + fa[h].reshape(256, 512)
     tasks = {
-        2: [lambda: red_b.pass_on(3)],
-        6: [red_c.middle],
-        10: [red_b.end, gat_b.start],
-        18: [lambda: gat_b.pass_on(1)],
-        25: [red_c.across, lambda: gat_b.pass_on(2)],
-        33: [lambda: red_c.pass_on(1), lambda: gat_b.pass_on(3)],
-        41: [gat_b.middle, lambda: red_c.pass_on(2)],
-        50: [lambda: red_c.pass_on(3)],
-        58: [gat_b.last, red_c.end],
+        4: (red_c, 1), 8: (gat_b, 1), 12: (red_c, 2), 17: (gat_b, 2), 21: (red_c, 3), 26: (gat_b, 3),
+        30: (red_c, 4), 36: (gat_b, 4), 41: (red_c, 5), 48: (gat_b, 5), 56: (red_c, 6),
     }
 
     def serve(point):
-        for task in tasks.get(point, []):
-            task()
+        if point in tasks:
+            tasks[point][0](tasks[point][1])
 
     spd_inverse(inv_a, inv_d, serve=serve)
     P3 = split(-inv_a[...])
     u = dot3(split(sb[...].reshape(16, 768)[:, :512]), P3, MM)
     u3 = split(u)
-    gat_b.end()
+    gat_b(6)
     a01 = split(both(fb, slice(0, 512)))
     w13 = split(both(fb, slice(512, 768)))
     s = sc[...].reshape(16, 768)[:, :512] - dot3(u3, a01, NT)
@@ -460,7 +490,9 @@
     vm = lambda *shape: pltpu.VMEM(shape, F32)
 
     def reduce_set(w):
-        return [vm(2, 2, 64, w), vm(2, 64, w), vm(8, 2, 8, w), vm(2, 8, w)]
+        v = w // 2
+        return [vm(2, 2, 64, v), vm(2, 64, v), vm(8, 2, 8, v), vm(8, 128),
+                vm(2, 2, 8, v), vm(2, 8, v), vm(8, 2, 4, 8, v), vm(2, 4, 8, v), vm(2, 8, w)]
 
     spec = pl.BlockSpec(memory_space=pltpu.VMEM)
     return pl.pallas_call(
@@ -468,12 +500,12 @@
         out_shape=(jax.ShapeDtypeStruct((512, 256), F32), jax.ShapeDtypeStruct((512, 256), BF16)),
         in_specs=[pl.BlockSpec(memory_space=pltpu.SMEM)] + [spec] * 6,
         out_specs=(spec, spec),
-        scratch_shapes=[vm(2, 256, 512), vm(2, 256, 768), vm(2, 256, 768),
+        scratch_shapes=[vm(2, 4, 64, 512), vm(2, 4, 64, 768), vm(2, 4, 64, 768),
                         pltpu.VMEM((1024, 512), BF16), pltpu.VMEM((1024, 512), BF16)]
-        + reduce_set(512) + [vm(2, 256, 512)] + reduce_set(768) + [vm(2, 256, 768)] + reduce_set(768)
+        + reduce_set(512) + reduce_set(768) + reduce_set(768) + [vm(2, 4, 64, 512), vm(2, 4, 64, 768)]
         + [vm(2, 8, 768), vm(8, 8, 768), vm(8, 768), vm(2, 256, 768)]
         + [vm(512, 512), vm(128, 128), vm(512, 768)]
-        + [pltpu.SemaphoreType.DMA((112,)), pltpu.SemaphoreType.DMA((112,))],
+        + [pltpu.SemaphoreType.DMA((168,)), pltpu.SemaphoreType.DMA((168,))],
         compiler_params=pltpu.CompilerParams(collective_id=0, has_side_effects=True, vmem_limit_bytes=60 << 20),
     )(leaf_rows, observations, basis_root, basis_region, noise_weights.reshape(8, 128), root_prior, region_prior[0])
 

time: 148 us -> 141 us (0.953)
  Pallas kernels: 142 us -> 136 us
    pallas_call x1, Pallas kernels: 142 us -> 136 us  [estimate(): pl.pallas_call(main_kernel, out_shape=(jax.ShapeDtypeStruct((512, 256), F...]
where the time goes in v4:
time: 141 us
  Pallas kernels  136 us (96%)
  local copies, waits for them, and re-layouts  2.12 us (2%)
  matrix products  2.12 us (2%)
    pallas_call x1, Pallas kernels, estimate(): pl.pallas_call(main_kernel, out_shape=(jax.ShapeDtypeStruct((512, 256), F...  136 us

profile of v4, /device:TPU:1, one launch (start us, length us, event | category | flops | bytes accessed | tf_op | source)
XLA Modules:
  0.0 141.2 jit_solution(6323783492011055785)
XLA Ops:
  1.3 0.0 copy-start
  1.3 135.6 %shard_map.86 = (f32[512,256]{1,0:T(8,128)}, bf16[512,256]{1,0:T(8,128)(2,1)}) custom-call(s32[1]{0:T(128)S(6)} %copy.11.rows_ref, bf16[1024,256]{1,0:T(8,128)(2,1)} %obs.1, bf16[1024,512]{1,0:T(8,128)(2,1)} %b0.1, bf16[1024,512]{1,0:T(8,128)(2,1)} %b1.1, f32[8,128]{1,0:T(8,128)} %bitcast.8, f32[512,512]{1,0:T(8,128)} %root_prior.1, f32[512,512]{1,0:T(8,128)} %bitcast.7), custom_call_target="tpu_custom_call" | custom-call | tf_op jit(solution)/shard_map/pallas_call | solution.py:498
  136.9 0.0 copy-done
  136.9 0.0 copy-start.1
  136.9 0.0 copy-start.3
  137.0 1.6 %fusion.1 = f32[256,1024]{1,0:T(8,128)S(1)} fusion(bf16[1024,512]{1,0:T(8,128)(2,1)S(1)} %copy-done, f32[512,256]{1,0:T(8,128)} %get-tuple-element.11), kind=kOutput, calls=%fused_computation.2 | convolution fusion | flops 268566528 | bytes 2621440 | tf_op jit(solution)/shard_map/dot_general | solution.py:519
  138.6 0.0 copy-done.1
  138.6 0.0 copy-done.3
  138.6 0.5 fusion
  139.1 0.0 copy-start.2
  139.1 1.3 copy.9
  140.4 0.0 copy-done.2
  140.4 0.8 copy.12
Async XLA Ops:
  1.3 135.6 %copy-start = (bf16[1024,512]{1,0:T(8,128)(2,1)S(1)}, bf16[1024,512]{1,0:T(8,128)(2,1)}, u32[]{:S(2)}) copy-start(bf16[1024,512]{1,0:T(8,128)(2,1)} %b0.1) | copy-start | bytes 3145732
  136.9 1.7 %copy-start.1 = (bf16[1024,512]{1,0:T(8,128)(2,1)S(1)}, bf16[1024,512]{1,0:T(8,128)(2,1)}, u32[]{:S(2)}) copy-start(bf16[1024,512]{1,0:T(8,128)(2,1)} %b1.1) | copy-start | bytes 3145732
  136.9 1.7 %copy-start.3 = (bf16[512,256]{1,0:T(8,128)(2,1)S(1)}, bf16[512,256]{1,0:T(8,128)(2,1)}, u32[]{:S(2)}) copy-start(bf16[512,256]{1,0:T(8,128)(2,1)} %get-tuple-element.5) | copy-start | bytes 786436
  139.1 1.3 copy-start.2

commit v5 on v4

--- a/solution.py
+++ b/solution.py
@@ -381,12 +381,20 @@
 
 
 def main_kernel(
-    rows_ref, obs, b0, b1, noise, root_prior, region_prior, root_out, region_low,
-    xa, xb, xc, w0, w1, *rest,
+    rows_ref, obs_in, b0_in, b1, noise, root_prior_in, region_prior_in, root_out, region_low,
+    xa, xb, xc, w0, w1, obs, b0, root_prior, region_prior, load_sems, *rest,
 ):
     sets, rest = [rest[9 * i:9 * i + 9] for i in range(3)], rest[27:]
     fa, fb, slab, rx, own, full, inv_a, inv_d, x0, send_sems, recv_sems = rest
     sa, sb, sc = [refs[8] for refs in sets]
+    loads = [
+        pltpu.make_async_copy(source, target, load_sems.at[i])
+        for i, (source, target) in enumerate(
+            [(b0_in, b0), (obs_in, obs), (region_prior_in, region_prior), (root_prior_in, root_prior)]
+        )
+    ]
+    for load in loads:
+        load.start()
     me = Place()
     copies = Copies(send_sems, recv_sems)
     barrier = pltpu.get_barrier_semaphore()
@@ -397,13 +405,15 @@
 
     count = rows_ref[0]
     lane = lax.broadcasted_iota(jnp.int32, (1, 128), 1)
-    for g in range(8):
-        wrow = jnp.where(lane + 128 * g < count, noise[g:g + 1, :], 0.0)
-        wt = jnp.broadcast_to(wrow, (128, 128)).T
-        for q in range(4):
-            rows, cols = slice(128 * g, 128 * g + 128), slice(128 * q, 128 * q + 128)
-            w1[rows, cols] = (b1[rows, cols].astype(F32) * wt).astype(BF16)
-            w0[rows, cols] = (b0[rows, cols].astype(F32) * wt).astype(BF16)
+    def weigh(source, target):
+        for g in range(8):
+            wrow = jnp.where(lane + 128 * g < count, noise[g:g + 1, :], 0.0)
+            wt = jnp.broadcast_to(wrow, (128, 128)).T
+            for q in range(4):
+                rows, cols = slice(128 * g, 128 * g + 128), slice(128 * q, 128 * q + 128)
+                target[rows, cols] = (source[rows, cols].astype(F32) * wt).astype(BF16)
+
+    weigh(b1, w1)
 
     def dot(a, b):
         return lax.dot_general(a, b, (TN, ((), ())), preferred_element_type=F32)
@@ -433,6 +443,9 @@
     red_a, red_b, red_c = [reduction(x, refs) for x, refs in zip((xa, xb, xc), sets)]
     gat_a, gat_b = gathering(sa, fa), gathering(sb, fb)
     red_a(0)
+    loads[0].wait()
+    loads[1].wait()
+    weigh(b0, w0)
     for h, half in halves:
         put(xb, h, slice(0, 512), dot(w0[:, half], b1[...]))
         put(xb, h, slice(512, 768), dot(w1[:, half], obs[...]))
@@ -441,15 +454,17 @@
     for h, half in halves:
         put(xc, h, slice(0, 512), 0.5 * (dot(w0[:, half], b0[...]) + dot(b0[:, half], w0[...])))
         put(xc, h, slice(512, 768), dot(w0[:, half], obs[...]))
-    for step in (red_a, 2), (red_a, 3), (red_b, 1), (red_a, 4), (red_a, 5), (red_b, 2), (red_a, 6), (gat_a, 0), \
-            (red_b, 3), (gat_a, 1), (gat_a, 2), (red_b, 4), (gat_a, 3), (red_c, 0), (gat_a, 4), (red_b, 5), \
-            (gat_a, 5), (red_b, 6), (gat_b, 0), (gat_a, 6):
+    for step in (red_a, 2), (red_a, 3), (red_a, 4), (red_b, 1), (red_a, 5), (red_a, 6), (gat_a, 0), (red_b, 2), \
+            (gat_a, 1), (red_b, 3), (gat_a, 2), (gat_a, 3), (red_c, 0), (red_b, 4), (gat_a, 4), (red_b, 5), \
+            (gat_a, 5), (gat_a, 6):
         step[0](step[1])
+    loads[2].wait()
+    loads[3].wait()
     for h, half in halves:
         inv_a[half, :] = region_prior[half, :] + fa[h].reshape(256, 512)
     tasks = {
-        4: (red_c, 1), 8: (gat_b, 1), 12: (red_c, 2), 17: (gat_b, 2), 21: (red_c, 3), 26: (gat_b, 3),
-        30: (red_c, 4), 36: (gat_b, 4), 41: (red_c, 5), 48: (gat_b, 5), 56: (red_c, 6),
+        1: (red_b, 6), 2: (gat_b, 0), 4: (red_c, 1), 9: (gat_b, 1), 13: (red_c, 2), 18: (gat_b, 2), 22: (red_c, 3),
+        27: (gat_b, 3), 31: (red_c, 4), 36: (gat_b, 4), 41: (red_c, 5), 47: (gat_b, 5), 56: (red_c, 6),
     }
 
     def serve(point):
@@ -495,13 +510,16 @@
                 vm(2, 2, 8, v), vm(2, 8, v), vm(8, 2, 4, 8, v), vm(2, 4, 8, v), vm(2, 8, w)]
 
     spec = pl.BlockSpec(memory_space=pltpu.VMEM)
+    away = pl.BlockSpec(memory_space=pl.ANY)
     return pl.pallas_call(
         main_kernel,
         out_shape=(jax.ShapeDtypeStruct((512, 256), F32), jax.ShapeDtypeStruct((512, 256), BF16)),
-        in_specs=[pl.BlockSpec(memory_space=pltpu.SMEM)] + [spec] * 6,
+        in_specs=[pl.BlockSpec(memory_space=pltpu.SMEM), away, away, spec, spec, away, away],
         out_specs=(spec, spec),
         scratch_shapes=[vm(2, 4, 64, 512), vm(2, 4, 64, 768), vm(2, 4, 64, 768),
-                        pltpu.VMEM((1024, 512), BF16), pltpu.VMEM((1024, 512), BF16)]
+                        pltpu.VMEM((1024, 512), BF16), pltpu.VMEM((1024, 512), BF16),
+                        pltpu.VMEM((1024, 256), BF16), pltpu.VMEM((1024, 512), BF16), vm(512, 512), vm(512, 512),
+                        pltpu.SemaphoreType.DMA((4,))]
         + reduce_set(512) + reduce_set(768) + reduce_set(768) + [vm(2, 4, 64, 512), vm(2, 4, 64, 768)]
         + [vm(2, 8, 768), vm(8, 8, 768), vm(8, 768), vm(2, 256, 768)]
         + [vm(512, 512), vm(128, 128), vm(512, 768)]

time: 141 us -> 142 us (level)
  no operation moved by 1% of the time
where the time goes in v5:
time: 142 us; the launch traced here: 141 us
  Pallas kernels  136 us (96%)
  local copies, waits for them, and re-layouts  2.12 us (1%)
  matrix products  2.12 us (1%)
    pallas_call x1, Pallas kernels, estimate(): pl.pallas_call(main_kernel, out_shape=(jax.ShapeDtypeStruct((512, 256), F...  136 us

profile of v5, /device:TPU:1, one launch (start us, length us, event | category | flops | bytes accessed | tf_op | source)
XLA Modules:
  0.0 141.4 jit_solution(12183723599648628692)
XLA Ops:
  1.3 0.0 copy-start
  1.3 135.8 %shard_map.86 = (f32[512,256]{1,0:T(8,128)}, bf16[512,256]{1,0:T(8,128)(2,1)}) custom-call(s32[1]{0:T(128)S(6)} %copy.11.rows_ref, bf16[1024,256]{1,0:T(8,128)(2,1)} %obs_in.1, bf16[1024,512]{1,0:T(8,128)(2,1)} %b0_in.1, bf16[1024,512]{1,0:T(8,128)(2,1)} %b1.1, f32[8,128]{1,0:T(8,128)} %bitcast.8, f32[512,512]{1,0:T(8,128)} %root_prior_in.1, f32[512,512]{1,0:T(8,128)} %bitcast.7), custom_call_target="tpu_custom_call" | custom-call | tf_op jit(solution)/shard_map/pallas_call | solution.py:514
  137.1 0.0 copy-done
  137.1 0.0 copy-start.1
  137.2 0.0 copy-start.3
  137.2 1.6 %fusion.1 = f32[256,1024]{1,0:T(8,128)S(1)} fusion(bf16[1024,512]{1,0:T(8,128)(2,1)S(1)} %copy-done, f32[512,256]{1,0:T(8,128)} %get-tuple-element.11), kind=kOutput, calls=%fused_computation.2 | convolution fusion | flops 268566528 | bytes 2621440 | tf_op jit(solution)/shard_map/dot_general | solution.py:537
  138.8 0.0 copy-done.1
  138.8 0.0 copy-done.3
  138.8 0.5 fusion
  139.3 0.0 copy-start.2
  139.3 1.3 copy.9
  140.6 0.0 copy-done.2
  140.6 0.8 copy.12
Async XLA Ops:
  1.3 135.9 %copy-start = (bf16[1024,512]{1,0:T(8,128)(2,1)S(1)}, bf16[1024,512]{1,0:T(8,128)(2,1)}, u32[]{:S(2)}) copy-start(bf16[1024,512]{1,0:T(8,128)(2,1)} %b0_in.1) | copy-start | bytes 3145732
  137.1 1.7 %copy-start.1 = (bf16[1024,512]{1,0:T(8,128)(2,1)S(1)}, bf16[1024,512]{1,0:T(8,128)(2,1)}, u32[]{:S(2)}) copy-start(bf16[1024,512]{1,0:T(8,128)(2,1)} %b1.1) | copy-start | bytes 3145732
  137.2 1.7 %copy-start.3 = (bf16[512,256]{1,0:T(8,128)(2,1)S(1)}, bf16[512,256]{1,0:T(8,128)(2,1)}, u32[]{:S(2)}) copy-start(bf16[512,256]{1,0:T(8,128)(2,1)} %get-tuple-element.5) | copy-start | bytes 786436
  139.3 1.3 copy-start.2
